TPU v7x, 256 devices: a whole 4x4x8 slice. The times are simulated.
256 devices in a mesh: row: 32 (over z, x), col: 8 (over y, core).
Axes of the slice: x: 4, y: 4, z: 8, core: 2. Of those that a mesh axis runs over, the one named last changes fastest.
Arguments:
- displacement: float32 [3, 256, 4, 128], P(None, ('row', 'col')), may hold values from -6 to 6
- load: float32 [3, 256, 4, 128], P(None, ('row', 'col')), may hold values from -6 to 6
- elastic_tangent: bfloat16 [21, 8, 256, 4, 128], P(None, None, ('row', 'col')), may hold values from -4 to 4
- band_flags: int32 [8, 256, 4, 128], P(None, ('row', 'col')), may hold values from 0 to 1, as said below
- contact_stiffness: bfloat16 [8192, 8, 2048], P(('row', 'col')), may hold values from 0.29882812 to 3
- normals: float32 [3, 8, 2048], replicated, as said below
- branch_length: float32 [8, 2048], replicated, may hold values from 0.5 to 2
- neighbours: int32 [8, 2048], replicated, may hold values from 0 to 2047, as said below
Outputs:
- residual: float32 [3, 256, 4, 128], P(None, ('row', 'col'))
- stress: float32 [6, 8, 256, 4, 128], P(None, None, ('row', 'col'))
- band_tangent: float32 [21, 8192], P(None, ('row', 'col'))
- band_stress: float32 [6, 8192], P(None, ('row', 'col'))
Inputs may be any that keep to these rules, and one draw needn't show every extreme that they name: `band_flags`: each block of 1 x-planes holds at most 32 flagged points, some blocks exactly 32; slots of contact_stiffness past a block's count are unused. `normals`: unit vectors. `neighbours`: every grain names at least 4 other grains; unused contact slots name the grain itself.
All inputs are finite; a program needn't handle non-finite values.
Results may differ from a plain program's by a relative error of at most 0.0003.
Values sent between devices are 32-bit elements; how exact they have to be, the bound alone decides.
No kernel may reach another device: no remote copies, remote signals or barrier semaphores. Data moves between devices by JAX's collectives and lax.ppermute only.
A program may use at most 128 MiB of HBM per device.

v0:
```python
import jax
import jax.numpy as jnp
import numpy as np
from jax import lax
from jax.sharding import PartitionSpec as P

SWEEPS = 4


RELAX_FACTOR = 0.8


def shifted(value, axis, steps):
    count = lax.axis_size(axis)
    leading, last = (max(0, -steps), min(count, count - steps))
    return lax.ppermute(value, axis, [(source, source + steps) for source in range(leading, last)])


def shape_table():
    low_point = 0.5 - 0.5 / np.sqrt(3.0)
    high_point = 0.5 + 0.5 / np.sqrt(3.0)
    deriv_table = np.zeros((8, 8, 3))
    for corner in range(8):
        corner_bits = [corner >> 2 & 1, corner >> 1 & 1, corner & 1]
        for gauss_id in range(8):
            gauss_bits = [gauss_id >> 2 & 1, gauss_id >> 1 & 1, gauss_id & 1]
            coords = [high_point if flag_bit else low_point for flag_bit in gauss_bits]
            values = [
                coords[axis_id] if corner_bits[axis_id] else 1.0 - coords[axis_id]
                for axis_id in range(3)
            ]
            slopes = [1.0 if corner_bits[axis_id] else -1.0 for axis_id in range(3)]
            for axis_id in range(3):
                product = slopes[axis_id]
                for other_axis in range(3):
                    if other_axis != axis_id:
                        product = product * values[other_axis]
                deriv_table[corner, gauss_id, axis_id] = product
    return jnp.asarray(deriv_table, jnp.float32)


def pair_list():
    return [(row_id, col_id) for row_id in range(6) for col_id in range(row_id, 6)]


def corner_values(padded, size_x, size_y, size_z):
    pieces = []
    for corner in range(8):
        shift_x, shift_y, shift_z = (corner >> 2 & 1, corner >> 1 & 1, corner & 1)
        pieces.append(
            padded[
                :,
                shift_x : shift_x + size_x,
                shift_y : shift_y + size_y,
                shift_z : shift_z + size_z,
            ]
        )
    return jnp.stack(pieces, axis=1)


def gauss_strains(corners):
    gradient = jnp.einsum(
        "iaxyz,agj->ijgxyz", corners, shape_table(), precision=lax.Precision.HIGHEST
    )
    return jnp.stack(
        [
            gradient[0, 0],
            gradient[1, 1],
            gradient[2, 2],
            gradient[1, 2] + gradient[2, 1],
            gradient[0, 2] + gradient[2, 0],
            gradient[0, 1] + gradient[1, 0],
        ]
    )


def elastic_stress(packed, strain):
    pairs = pair_list()
    result_rows = []
    for row_id in range(6):
        running = jnp.zeros_like(strain[0])
        for col_id in range(6):
            position = pairs.index((min(row_id, col_id), max(row_id, col_id)))
            running = running + packed[position].astype(jnp.float32) * strain[col_id]
        result_rows.append(running)
    return jnp.stack(result_rows)


def nodal_forces(stress):
    voigt_rows = [[0, 5, 4], [5, 1, 3], [4, 3, 2]]
    tensor = jnp.stack(
        [jnp.stack([stress[comp_id] for comp_id in row_list]) for row_list in voigt_rows]
    )
    return 0.125 * jnp.einsum(
        "ijgxyz,agj->iaxyz", tensor, shape_table(), precision=lax.Precision.HIGHEST
    )


def assemble(corner_forces):
    summed = None
    for corner in range(8):
        shift_x, shift_y, shift_z = (corner >> 2 & 1, corner >> 1 & 1, corner & 1)
        placed = jnp.pad(
            corner_forces[:, corner],
            ((0, 0), (shift_x, 1 - shift_x), (shift_y, 1 - shift_y), (shift_z, 1 - shift_z)),
        )
        summed = placed if summed is None else summed + placed
    return summed


def contact_template(normals, neighbours):
    grain_total = neighbours.shape[1]
    contact_mask = (neighbours != jnp.arange(grain_total, dtype=jnp.int32)[None, :]).astype(
        jnp.float32
    )
    projector = jnp.stack(
        [
            normals[0] * normals[0],
            normals[1] * normals[1],
            normals[2] * normals[2],
            normals[1] * normals[2],
            normals[0] * normals[2],
            normals[0] * normals[1],
        ]
    )
    return (contact_mask, projector)


def relax_rve(strain_row, stiffness, normals, branch_length, neighbours, contact_mask, projector):
    grain_total = neighbours.shape[1]
    weights = stiffness * contact_mask
    affine = branch_length * jnp.sum(strain_row[:, None, None] * projector, axis=0)
    diagonal = jnp.sum(weights, axis=0)
    fluctuation = jnp.zeros((3, grain_total), jnp.float32)
    for sweep_id in range(SWEEPS):
        stretch = affine + jnp.sum(
            normals * (fluctuation[:, neighbours] - fluctuation[:, None, :]), axis=0
        )
        unbalanced = jnp.sum(normals * (weights * stretch)[None], axis=1)
        fluctuation = fluctuation + RELAX_FACTOR * unbalanced / diagonal[None, :]
    stretch = affine + jnp.sum(
        normals * (fluctuation[:, neighbours] - fluctuation[:, None, :]), axis=0
    )
    contact_force = (weights * stretch * branch_length).reshape(-1)
    flat_proj = projector.reshape(6, -1)
    stress_row = jnp.dot(flat_proj, contact_force, precision=lax.Precision.HIGHEST) / grain_total
    stiff_term = (weights * branch_length * branch_length).reshape(-1)
    full = (
        jnp.dot(flat_proj * stiff_term[None, :], flat_proj.T, precision=lax.Precision.HIGHEST)
        / grain_total
    )
    tangent_row = jnp.stack([full[row_id, col_id] for row_id, col_id in pair_list()])
    return (stress_row, tangent_row)


def run_slots(strain_rows, stiffness_stack, live_order, live_total, template):
    slot_total = strain_rows.shape[0]
    batch_size = min(8, slot_total)
    relax_many = jax.vmap(relax_rve, in_axes=(0, 0, None, None, None, None, None))
    lane_ids = jnp.arange(batch_size, dtype=jnp.int32)

    def step_fn(batch_id, results_pair):
        stress_rows, tangent_rows = results_pair
        positions = batch_id * batch_size + lane_ids
        valid_lane = positions < live_total
        picked_rows = live_order[jnp.minimum(positions, slot_total - 1)]
        many_stress, many_tangent = relax_many(
            strain_rows[picked_rows], stiffness_stack[picked_rows], *template
        )
        target_rows = jnp.where(valid_lane, picked_rows, slot_total)
        return (
            stress_rows.at[target_rows].set(many_stress),
            tangent_rows.at[target_rows].set(many_tangent),
        )

    initial = (
        jnp.zeros((slot_total + 1, 6), jnp.float32),
        jnp.zeros((slot_total + 1, 21), jnp.float32),
    )
    turn_count = (live_total + batch_size - 1) // batch_size
    stress_rows, tangent_rows = lax.fori_loop(0, turn_count, step_fn, initial)
    return (stress_rows[:slot_total], tangent_rows[:slot_total])


def body(
    displacement,
    load,
    elastic_tangent,
    band_flags,
    contact_stiffness,
    normals,
    branch_length,
    neighbours,
):
    planes, size_y, size_z = (displacement.shape[1], displacement.shape[2], displacement.shape[3])
    upper_rim = shifted(displacement, ("row", "col"), -1)
    padded = jnp.concatenate([displacement, upper_rim], axis=1)
    padded = jnp.pad(padded, ((0, 0), (0, 0), (0, 1), (0, 1)))
    strain = gauss_strains(corner_values(padded, planes, size_y, size_z))
    elastic = elastic_stress(elastic_tangent, strain)
    points = 8 * planes * size_y * size_z
    strain_flat = strain.reshape(6, points)
    flags_flat = band_flags.reshape(points)
    slot_count = contact_stiffness.shape[0]
    slot_ids = jnp.arange(slot_count, dtype=jnp.int32)
    flag_rank = jnp.cumsum(flags_flat) - 1
    select = ((flag_rank[None, :] == slot_ids[:, None]) & (flags_flat[None, :] == 1)).astype(
        jnp.float32
    )
    slot_strain = jnp.dot(select, strain_flat.T, precision=lax.Precision.HIGHEST)
    live_count = jnp.sum(flags_flat)
    contact_mask, projector = contact_template(normals, neighbours)
    template = (normals, branch_length, neighbours, contact_mask, projector)
    line_size = lax.axis_size("row")
    offset = lax.axis_index("row")
    per_peer = -(-slot_count // line_size)
    dest_ids = jnp.arange(line_size, dtype=jnp.int32)[:, None]
    peer_slots = jnp.arange(per_peer, dtype=jnp.int32)[None, :]
    item_index = (dest_ids - offset) % line_size + peer_slots * line_size
    live_send = (item_index < live_count).astype(jnp.float32)
    clipped = jnp.minimum(item_index, slot_count - 1)
    stiff_send = contact_stiffness[clipped].astype(jnp.float32)
    strain_send = slot_strain[clipped]
    stiff_recv = lax.all_to_all(stiff_send, "row", split_axis=0, concat_axis=0, tiled=True)
    strain_recv = lax.all_to_all(strain_send, "row", split_axis=0, concat_axis=0, tiled=True)
    live_recv = lax.all_to_all(live_send, "row", split_axis=0, concat_axis=0, tiled=True)
    sources = live_recv.shape[0]
    items = live_recv.shape[1]
    flat_items = sources * items
    live_int = (live_recv.reshape(flat_items) > 0.5).astype(jnp.int32)
    live_order = jnp.argsort(1 - live_int, stable=True)
    live_total = jnp.sum(live_int)
    stiff_rows = stiff_recv.reshape((flat_items,) + stiff_recv.shape[2:])
    strain_rows = strain_recv.reshape(flat_items, 6)
    out_stress, out_tangent = run_slots(strain_rows, stiff_rows, live_order, live_total, template)
    back_stress = lax.all_to_all(
        out_stress.reshape(sources, items, 6), "row", split_axis=0, concat_axis=0, tiled=True
    )
    back_tangent = lax.all_to_all(
        out_tangent.reshape(sources, items, 21), "row", split_axis=0, concat_axis=0, tiled=True
    )
    home_dest = (offset + slot_ids) % line_size
    home_slot = slot_ids // line_size
    live = (slot_ids < live_count)[:, None]
    slot_stress = jnp.where(live, back_stress[home_dest, home_slot], 0.0)
    slot_tangent = jnp.where(live, back_tangent[home_dest, home_slot], 0.0)
    band_part = jnp.dot(slot_stress.T, select, precision=lax.Precision.HIGHEST)
    stress_flat = jnp.where(flags_flat[None, :] == 1, band_part, elastic.reshape(6, points))
    stress = stress_flat.reshape(6, 8, planes, size_y, size_z)
    summed = assemble(nodal_forces(stress))
    carried = summed[:, planes : planes + 1, :size_y, :size_z]
    arrived = shifted(carried, ("row", "col"), 1)
    owned = summed[:, :planes, :size_y, :size_z]
    owned = owned.at[:, 0:1].add(arrived)
    residual = load - owned
    return (residual, stress, slot_tangent.T, slot_stress.T)


def solution(mesh):
    placed = (
        P(None, ("row", "col"), None, None),
        P(None, ("row", "col"), None, None),
        P(None, None, ("row", "col"), None, None),
        P(None, ("row", "col"), None, None),
        P(("row", "col"), None, None),
        P(),
        P(),
        P(),
    )
    return jax.shard_map(
        body,
        mesh=mesh,
        in_specs=placed,
        out_specs=(
            P(None, ("row", "col"), None, None),
            P(None, None, ("row", "col"), None, None),
            P(None, ("row", "col")),
            P(None, ("row", "col")),
        ),
        check_vma=False,
    )
```

profile of v0, /device:TPU:128, one launch (start us, length us, event | category | flops | bytes accessed | tf_op | source)
XLA Modules:
  0.0 2180.9 jit_solution(17220993237171807500)
XLA Ops:
  0.7 6.2 collective-permute-start
  9.6 8.1 all-to-all-start
  26.3 9.8 all-to-all-start.2
  37.7 3.2 all-to-all-done.2
  40.9 9.5 all-to-all-start.1
  50.4 4.6 copy.578
  63.6 30.8 %all-to-all-done.1 = f32[32,1,8,2048]{3,2,1,0:T(8,128)} async-done(((f32[32,1,8,2048]{3,2,1,0:T(8,128)}), f32[32,1,8,2048]{3,2,1,0:T(8,128)}, u32[]{:S(2)}, u32[]{:S(2)}) %all-to-all-start.1) | async-done | bytes 2097184 | tf_op jit(solution)/shard_map/all_to_all | solution.py:224
  95.1 1363.8 %while.15 = (s32[]{:T(128)}, f32[33,6]{1,0:T(8,128)}, f32[33,21]{1,0:T(8,128)S(1)}, s32[]{:T(128)}, s32[]{:T(128)}, /*index=5*/s32[32]{0:T(128)S(1)}, f32[32,8,2...) while((s32[]{:T(128)}, f32[33,6]{1,0:T(8,128)}, ...), condition=%wide.region_19.20_spmd.clone, body=%wide.region_5.19_spmd.clone.sunk | while | flops 79481280 | bytes 63311232 | solution.py:181
  97.0 5.2 copy.765
  102.9 2.2 gather_fusion.1
  105.5 20.7 fusion.131
  128.8 54.4 %gather_fusion.2 = f32[16384,3]{1,0:T(8,128)} fusion(f32[3,2048]{0,1:T(8,128)S(1)} %broadcast.752, s32[16384]{0:T(1024)S(1)} %broadcast_clamp_fusion.2), kind=kCustom, calls=%fused_computation.3.clone.clone.1 | custom fusion | bytes 458752 | tf_op jit(solution)/shard_map/while/body/vmap()/gather | solution.py:137
  183.2 8.0 multiply_reduce_fusion.14
  192.0 3.1 copy.766
  195.1 121.2 %gather_fusion.4 = f32[16384,8,3]{1,2,0:T(4,128)} fusion(f32[8,3,2048]{0,1,2:T(4,128)} %copy.766, s32[16384]{0:T(1024)S(1)} %broadcast_clamp_fusion.2), kind=kCustom, calls=%fused_computation.4.clone.clone.1 | custom fusion | bytes 3211264 | tf_op jit(solution)/shard_map/while/body/vmap()/gather | solution.py:137
  316.3 18.9 copy.767
  337.6 3.1 copy.768
  340.7 121.2 %gather_fusion.5 = f32[16384,8,3]{1,2,0:T(4,128)} fusion(f32[8,3,2048]{0,1,2:T(4,128)} %copy.768, s32[16384]{0:T(1024)S(1)} %broadcast_clamp_fusion.2), kind=kCustom, calls=%fused_computation.5.clone.clone.1 | custom fusion | bytes 3211264 | tf_op jit(solution)/shard_map/while/body/vmap()/gather | solution.py:137
  461.9 18.9 copy.769
  483.2 3.1 copy.770
  486.2 121.2 %gather_fusion.6 = f32[16384,8,3]{1,2,0:T(4,128)} fusion(f32[8,3,2048]{0,1,2:T(4,128)} %copy.770, s32[16384]{0:T(1024)S(1)} %broadcast_clamp_fusion.2), kind=kCustom, calls=%fused_computation.6.clone.clone.1 | custom fusion | bytes 3211264 | tf_op jit(solution)/shard_map/while/body/vmap()/gather | solution.py:137
  607.5 18.9 copy.771
  628.7 3.1 copy.772
  631.8 121.2 %gather_fusion.7 = f32[16384,8,3]{1,2,0:T(4,128)} fusion(f32[8,3,2048]{0,1,2:T(4,128)} %copy.772, s32[16384]{0:T(1024)S(1)} %broadcast_clamp_fusion.2), kind=kCustom, calls=%fused_computation.7.clone.clone.1 | custom fusion | bytes 3211264 | tf_op jit(solution)/shard_map/while/body/vmap()/gather | solution.py:142
  753.0 18.9 copy.773
  775.1 1.9 scatter_fusion
  778.9 5.2 copy.765
  784.9 2.2 gather_fusion.1
  787.4 20.7 fusion.131
  810.7 54.4 %gather_fusion.2 = f32[16384,3]{1,0:T(8,128)} fusion(f32[3,2048]{0,1:T(8,128)S(1)} %broadcast.752, s32[16384]{0:T(1024)S(1)} %broadcast_clamp_fusion.2), kind=kCustom, calls=%fused_computation.3.clone.clone.1 | custom fusion | bytes 458752 | tf_op jit(solution)/shard_map/while/body/vmap()/gather | solution.py:137
  865.2 8.0 multiply_reduce_fusion.14
  873.9 3.1 copy.766
  877.0 121.2 %gather_fusion.4 = f32[16384,8,3]{1,2,0:T(4,128)} fusion(f32[8,3,2048]{0,1,2:T(4,128)} %copy.766, s32[16384]{0:T(1024)S(1)} %broadcast_clamp_fusion.2), kind=kCustom, calls=%fused_computation.4.clone.clone.1 | custom fusion | bytes 3211264 | tf_op jit(solution)/shard_map/while/body/vmap()/gather | solution.py:137
  998.2 18.9 copy.767
  1019.5 3.1 copy.768
  1022.6 121.2 %gather_fusion.5 = f32[16384,8,3]{1,2,0:T(4,128)} fusion(f32[8,3,2048]{0,1,2:T(4,128)} %copy.768, s32[16384]{0:T(1024)S(1)} %broadcast_clamp_fusion.2), kind=kCustom, calls=%fused_computation.5.clone.clone.1 | custom fusion | bytes 3211264 | tf_op jit(solution)/shard_map/while/body/vmap()/gather | solution.py:137
  1143.8 18.9 copy.769
  1165.1 3.1 copy.770
  1168.1 121.2 %gather_fusion.6 = f32[16384,8,3]{1,2,0:T(4,128)} fusion(f32[8,3,2048]{0,1,2:T(4,128)} %copy.770, s32[16384]{0:T(1024)S(1)} %broadcast_clamp_fusion.2), kind=kCustom, calls=%fused_computation.6.clone.clone.1 | custom fusion | bytes 3211264 | tf_op jit(solution)/shard_map/while/body/vmap()/gather | solution.py:137
  1289.4 18.9 copy.771
  1310.6 3.1 copy.772
  1313.7 121.2 %gather_fusion.7 = f32[16384,8,3]{1,2,0:T(4,128)} fusion(f32[8,3,2048]{0,1,2:T(4,128)} %copy.772, s32[16384]{0:T(1024)S(1)} %broadcast_clamp_fusion.2), kind=kCustom, calls=%fused_computation.7.clone.clone.1 | custom fusion | bytes 3211264 | tf_op jit(solution)/shard_map/while/body/vmap()/gather | solution.py:142
  1434.9 18.9 copy.773
  1457.0 1.9 scatter_fusion
  1460.3 690.1 %all-to-all-start.3 = ((f32[32,1,6]{2,1,0:T(1,128)}), f32[32,1,6]{2,1,0:T(1,128)S(1)}, u32[]{:S(2)}, u32[]{:S(2)}) async-start(f32[32,1,6]{2,1,0:T(1,128)} %bitcast.38), calls=%async_computation.3 | async-start | bytes 32768 | tf_op jit(solution)/shard_map/all_to_all | solution.py:236
  2155.7 9.8 all-to-all-start.4
  2169.9 1.9 collective-permute-start.1
  2173.2 7.1 collective-permute-done.1
  (255 shorter events, 67.0 us)
Async XLA Ops:
  0.6 22.1 %copy-start = (bf16[32,8,2048]{2,1,0:T(8,128)(2,1)S(1)}, bf16[32,8,2048]{2,1,0:T(8,128)(2,1)}, u32[]{:S(2)}) copy-start(bf16[32,8,2048]{2,1,0:T(8,128)(2,1)} %param.20) | copy-start | bytes 3145732
  0.6 23.0 %copy-start.22 = (f32[8,8,3,1,1]{0,1,4,3,2:T(8,128)S(1)}, f32[8,8,3,1,1]{0,1,4,3,2:T(8,128)}, u32[]{:S(2)}) copy-start(f32[8,8,3,1,1]{0,1,4,3,2:T(8,128)} %constant.195) | copy-start | bytes 2308
  0.7 22.8 %copy-start.19 = (f32[3,1,4,128]{3,2,1,0:T(4,128)S(1)}, f32[3,1,4,128]{3,2,1,0:T(4,128)}, u32[]{:S(2)}) copy-start(f32[3,1,4,128]{3,2,1,0:T(4,128)} %param.16) | copy-start | bytes 18436
  0.7 22.7 %collective-permute-start = (f32[3,1,4,128]{3,2,0,1:T(4,128)}, f32[3,1,4,128]{3,2,0,1:T(4,128)S(1)}, u32[]{:S(2)}, u32[]{:S(2)}) collective-permute-start(f32[3,1,4,128]{3,2,0,1:T(4,128)} %bitcast.434), channel_id=1, source_target_pairs={{1,0},{2,1},{3,2},{4,3},{5,4},{6,5},{7,6},{8,7},{9,8},{10,9},{11,1... | collective-permute-start | bytes 18440 | tf_op jit(solution)/shard_map/ppermute | solution.py:16
  9.6 16.8 all-to-all-start
  19.1 5.7 copy-start.24
  21.4 3.2 copy-start.11
  21.4 39.7 %copy-start.15 = (bf16[1,8,1,4,128]{4,3,2,1,0:T(4,128)(2,1)}, bf16[1,8,1,4,128]{4,3,2,1,0:T(4,128)(2,1)S(1)}, u32[]{:S(2)}) copy-start(bf16[1,8,1,4,128]{4,3,2,1,0:T(4,128)(2,1)S(1)} %get-tuple-element.310) | copy-start | bytes 24580
  21.4 40.3 %copy-start.14 = (bf16[1,8,1,4,128]{4,3,2,1,0:T(4,128)(2,1)}, bf16[1,8,1,4,128]{4,3,2,1,0:T(4,128)(2,1)S(1)}, u32[]{:S(2)}) copy-start(bf16[1,8,1,4,128]{4,3,2,1,0:T(4,128)(2,1)S(1)} %get-tuple-element.309) | copy-start | bytes 24580
  21.4 41.0 %copy-start.13 = (bf16[1,8,1,4,128]{4,3,2,1,0:T(4,128)(2,1)}, bf16[1,8,1,4,128]{4,3,2,1,0:T(4,128)(2,1)S(1)}, u32[]{:S(2)}) copy-start(bf16[1,8,1,4,128]{4,3,2,1,0:T(4,128)(2,1)S(1)} %get-tuple-element.308) | copy-start | bytes 24580
  21.4 41.6 %copy-start.16 = (bf16[1,8,1,4,128]{4,3,2,1,0:T(4,128)(2,1)}, bf16[1,8,1,4,128]{4,3,2,1,0:T(4,128)(2,1)S(1)}, u32[]{:S(2)}) copy-start(bf16[1,8,1,4,128]{4,3,2,1,0:T(4,128)(2,1)S(1)} %get-tuple-element.311) | copy-start | bytes 24580
  22.7 2.0 copy-start.20
  23.9 39.1 %copy-start.3 = (f32[3,3,8,1,4,128]{5,2,4,0,1,3:T(8,128)}, f32[3,3,8,1,4,128]{5,2,4,0,1,3:T(8,128)S(1)}, u32[]{:S(2)}) copy-start(f32[3,3,8,1,4,128]{5,2,4,0,1,3:T(8,128)S(1)} %convolution_bitcast_fusion.1) | copy-start | bytes 442372
  24.6 38.4 %copy-start.7 = (f32[1,1,8,1,4,128]{5,2,4,3,1,0:T(8,128)}, f32[1,1,8,1,4,128]{5,2,4,3,1,0:T(8,128)S(1)}, u32[]{:S(2)}) copy-start(f32[1,1,8,1,4,128]{5,2,4,3,1,0:T(8,128)S(1)} %get-tuple-element.262) | copy-start | bytes 49156
  24.6 38.4 %copy-start.8 = (f32[1,1,8,1,4,128]{5,2,4,3,1,0:T(8,128)}, f32[1,1,8,1,4,128]{5,2,4,3,1,0:T(8,128)S(1)}, u32[]{:S(2)}) copy-start(f32[1,1,8,1,4,128]{5,2,4,3,1,0:T(8,128)S(1)} %get-tuple-element.263) | copy-start | bytes 49156
  24.6 38.4 %copy-start.9 = (f32[1,1,8,1,4,128]{5,2,4,0,1,3:T(8,128)}, f32[1,1,8,1,4,128]{5,2,4,0,1,3:T(8,128)S(1)}, u32[]{:S(2)}) copy-start(f32[1,1,8,1,4,128]{5,2,4,0,1,3:T(8,128)S(1)} %get-tuple-element.264) | copy-start | bytes 49156
  26.3 14.6 all-to-all-start.2
  37.7 12.7 copy-start.10
  40.9 53.6 %all-to-all-start.1 = ((f32[32,1,8,2048]{3,2,1,0:T(8,128)}), f32[32,1,8,2048]{3,2,1,0:T(8,128)}, u32[]{:S(2)}, u32[]{:S(2)}) async-start(f32[32,1,8,2048]{3,2,1,0:T(8,128)} %bitcast_convert_fusion), calls=%async_computation.1 | async-start | bytes 4194304 | tf_op jit(solution)/shard_map/all_to_all | solution.py:224
  55.0 2.7 copy-start.4
  55.0 40.1 %copy-start.2 = (f32[8,2048]{1,0:T(8,128)S(1)}, f32[8,2048]{1,0:T(8,128)}, u32[]{:S(2)}) copy-start(f32[8,2048]{1,0:T(8,128)} %param.22) | copy-start | bytes 196612
  95.1 2055.4 %copy-start.12 = (bf16[1,8,1,4,128]{4,3,2,1,0:T(4,128)(2,1)S(1)}, bf16[1,8,1,4,128]{4,3,2,1,0:T(4,128)(2,1)}, u32[]{:S(2)}) copy-start(bf16[1,8,1,4,128]{4,3,2,1,0:T(4,128)(2,1)} %copy-done.11) | copy-start | bytes 24580
  95.1 2070.4 %copy-start.6 = (s32[32]{0:T(128)S(1)}, s32[32]{0:T(128)}, u32[]{:S(2)}) copy-start(s32[32]{0:T(128)} %fusion.85) | copy-start | bytes 388
  128.7 62.5 %copy-start.17 = (f32[33,21]{1,0:T(8,128)}, f32[33,21]{1,0:T(8,128)S(1)}, u32[]{:S(2)}) copy-start(f32[33,21]{1,0:T(8,128)S(1)} %scatter_custom_fusion.10) | copy-start | bytes 8320 | tf_op jit(solution)/shard_map/while
  773.6 3.4 copy-start.5
  773.6 3.4 copy-start.18
  810.6 62.5 %copy-start.17 = (f32[33,21]{1,0:T(8,128)}, f32[33,21]{1,0:T(8,128)S(1)}, u32[]{:S(2)}) copy-start(f32[33,21]{1,0:T(8,128)S(1)} %scatter_custom_fusion.10) | copy-start | bytes 8320 | tf_op jit(solution)/shard_map/while
  1455.5 3.4 copy-start.5
  1455.5 3.4 copy-start.18
  1458.9 709.2 %copy-start.21 = (f32[8,8,3,1,1]{0,1,2,4,3:T(8,128)S(1)}, f32[8,8,3,1,1]{0,1,2,4,3:T(8,128)}, u32[]{:S(2)}) copy-start(f32[8,8,3,1,1]{0,1,2,4,3:T(8,128)} %constant.196) | copy-start | bytes 2308
  1458.9 713.5 %copy-start.25 = (pred[32]{0:T(512)(128)(4,1)S(1)}, pred[32]{0:T(512)(128)(4,1)}, u32[]{:S(2)}) copy-start(pred[32]{0:T(512)(128)(4,1)} %iota_compare_fusion.4) | copy-start | bytes 100
  1458.9 721.4 %copy-start.23 = (f32[3,1,4,128]{3,2,1,0:T(4,128)S(1)}, f32[3,1,4,128]{3,2,1,0:T(4,128)}, u32[]{:S(2)}) copy-start(f32[3,1,4,128]{3,2,1,0:T(4,128)} %param.17) | copy-start | bytes 18436
  1458.9 722.0 %copy-start.1 = (bf16[32,8,2048]{2,1,0:T(8,128)(2,1)S(1)}, bf16[32,8,2048]{2,1,0:T(8,128)(2,1)}, u32[]{:S(2)}) copy-start(bf16[32,8,2048]{2,1,0:T(8,128)(2,1)} %param.20) | copy-start | bytes 3145732
  1460.3 695.3 %all-to-all-start.3 = ((f32[32,1,6]{2,1,0:T(1,128)}), f32[32,1,6]{2,1,0:T(1,128)S(1)}, u32[]{:S(2)}, u32[]{:S(2)}) async-start(f32[32,1,6]{2,1,0:T(1,128)} %bitcast.38), calls=%async_computation.3 | async-start | bytes 32768 | tf_op jit(solution)/shard_map/all_to_all | solution.py:236
  2155.7 16.1 all-to-all-start.4
  2169.9 10.4 collective-permute-start.1
where the time goes:
time: 2190 us; the launch traced here: 2180 us
  local copies, waits for them, and re-layouts  1300 us (59%)
  starting transfers between devices  735 us (34%)
  other arithmetic  54.6 us (2%)
  matrix products  46 us (2%)
  waiting for transfers between devices  41.1 us (2%)
    gather x18, local copies, waits for them, and re-layouts, relax_rve(): fluctuation[:, neighbours] - fluctuation[:, None, :]  1230 us
    all_to_all x1, starting transfers between devices, body(): lax.all_to_all(out_stress.reshape(sources, items, 6), 'row', split_axis=0...  690 us
  transfers between devices with their start and end apart: 7, of which 3 were waited for; matrix products, arithmetic and copies ran while one was open for 2% of the time, Pallas kernels for 0%

commit v1 on v0

v1 whole, which is shorter than its diff:
```python
import jax
import jax.numpy as jnp
import numpy as np
from jax import lax
from jax.experimental import pallas as pl
from jax.experimental.pallas import tpu as pltpu
from jax.sharding import PartitionSpec as P

SWEEPS = 4
RELAX_FACTOR = 0.8
LOW = float(0.5 - 0.5 / np.sqrt(3.0))
HIGH = float(0.5 + 0.5 / np.sqrt(3.0))
GRAINS = 2048
CONTACTS = 8
SLOT_COUNT = 32
GROUPS = SLOT_COUNT // 8
CHUNKS = GRAINS // 128
PAIRS = [(row_id, col_id) for row_id in range(6) for col_id in range(row_id, 6)]
NT = (((1,), (1,)), ((), ()))


def shifted(value, axis, steps):
    count = lax.axis_size(axis)
    leading, last = (max(0, -steps), min(count, count - steps))
    return lax.ppermute(value, axis, [(source, source + steps) for source in range(leading, last)])


def lanes_of(chunk):
    return pl.ds(pl.multiple_of(chunk * 128, 128), 128)


def row8(ref, row, lanes):
    return jnp.broadcast_to(ref[row : row + 1, lanes], (8, 128))


def take_lanes(table, index):
    return jnp.take_along_axis(table, index, axis=1, mode="promise_in_bounds")


def template_kernel(
    flags_ref,
    stiff_ref,
    nrm_ref,
    br_ref,
    nbr_ref,
    wt_ref,
    cd_ref,
    tan_ref,
    rank_ref,
    sel_ref,
    lp_ref,
    near_ref,
    raw_ref,
    basis_ref,
    high_ref,
    low_ref,
):
    flags = flags_ref[...]
    flags_f = flags.astype(jnp.float32)
    tri = (
        lax.broadcasted_iota(jnp.int32, (128, 128), 0)
        <= lax.broadcasted_iota(jnp.int32, (128, 128), 1)
    ).astype(jnp.float32)
    inside = jnp.dot(flags_f, tri, preferred_element_type=jnp.float32)
    before = (
        lax.broadcasted_iota(jnp.int32, (32, 32), 1) < lax.broadcasted_iota(jnp.int32, (32, 32), 0)
    ).astype(jnp.float32)
    ahead = jnp.sum(
        jnp.dot(before, flags_f, preferred_element_type=jnp.float32), axis=1, keepdims=True
    )
    rank = jnp.where(flags == 1, (inside + ahead - 1.0).astype(jnp.int32), -1)
    rank_ref[...] = rank
    live_total = jnp.sum(flags_f)
    slot_rows = lax.broadcasted_iota(jnp.int32, (32, 128), 0)
    for row in range(32):
        picked = jnp.broadcast_to(rank_ref[row : row + 1, :], (32, 128)) == slot_rows
        sel_ref[:, row * 128 : (row + 1) * 128] = jnp.where(picked, 1.0, 0.0).astype(jnp.bfloat16)

    basis_ref[168:256, :] = jnp.zeros((88, 128), jnp.float32)
    for chunk in range(CHUNKS):
        lanes = slice(chunk * 128, (chunk + 1) * 128)
        names = nbr_ref[:, lanes]
        own = lax.broadcasted_iota(jnp.int32, (8, 128), 1) + chunk * 128
        reach = (names - (chunk * 128 - 64)) & (GRAINS - 1)
        widest = jnp.max(reach.astype(jnp.float32))
        near_ref[chunk] = (widest < 256.0).astype(jnp.int32)

    def chunk_step(chunk, carry):
        lanes = lanes_of(chunk)
        names = nbr_ref[:, lanes]
        own = lax.broadcasted_iota(jnp.int32, (8, 128), 1) + chunk * 128
        mask = jnp.where(names != own, 1.0, 0.0)
        n0, n1, n2 = (nrm_ref[axis_id, :, lanes] for axis_id in range(3))
        length = br_ref[:, lanes]
        proj = [n0 * n0, n1 * n1, n2 * n2, n1 * n2, n0 * n2, n0 * n1]
        scaled = [length * value for value in proj]
        for comp in range(6):
            lp_ref[comp, :, lanes] = scaled[comp]
        for place, (row_id, col_id) in enumerate(PAIRS):
            basis_ref[place * 8 : (place + 1) * 8, :] = scaled[row_id] * scaled[col_id]
        for contact in range(CONTACTS):
            basis = basis_ref[pl.ds(contact, 32, stride=8), :]
            high = basis.astype(jnp.bfloat16)
            high_ref[contact, :, lanes] = high
            low_ref[contact, :, lanes] = (basis - high.astype(jnp.float32)).astype(jnp.bfloat16)
        for slot in range(SLOT_COUNT):
            raw_ref[slot * 8 : (slot + 1) * 8, :] = (
                stiff_ref[slot, :, lanes].astype(jnp.float32) * mask
            )
        for group in range(GROUPS):
            total = None
            for contact in range(CONTACTS):
                value = raw_ref[pl.ds(group * 64 + contact, 8, stride=8), :]
                wt_ref[contact, group * 8 : (group + 1) * 8, lanes] = value
                total = value if total is None else total + value
            cd_ref[group * 8 : (group + 1) * 8, lanes] = RELAX_FACTOR / total
        return carry

    lax.fori_loop(0, CHUNKS, chunk_step, 0)

    acc = jnp.zeros((32, 32), jnp.float32)
    for contact in range(CONTACTS):
        weights = wt_ref[contact].astype(jnp.bfloat16)
        for part_ref in (high_ref, low_ref):
            acc = acc + lax.dot_general(
                part_ref[contact], weights, NT, preferred_element_type=jnp.float32
            )
    slot_lane = lax.broadcasted_iota(jnp.int32, (32, 32), 1).astype(jnp.float32)
    acc = jnp.where(slot_lane < live_total, acc * (1.0 / GRAINS), 0.0)
    tan_ref[...] = acc[:21]


def lerp(low_value, high_value, bit):
    weight = HIGH if bit else LOW
    return low_value + weight * (high_value - low_value)


def strain_rows(plane_refs, dup_ref):
    row = lax.broadcasted_iota(jnp.int32, (8, 128), 0)
    lane = lax.broadcasted_iota(jnp.int32, (8, 128), 1)
    z_weight = jnp.where(row < 4, LOW, HIGH)
    last_y = (row & 3) == 3
    last_z = lane == 127
    gradient = {}
    for axis_id in range(3):
        along, slope = {}, {}
        for bit_x in range(2):
            plane = plane_refs[bit_x][axis_id]
            dup_ref[0:4, :] = plane
            dup_ref[4:8, :] = plane
            base = dup_ref[...]
            for bit_y in range(2):
                value = base if bit_y == 0 else jnp.where(last_y, 0.0, pltpu.roll(base, 7, 0))
                after = jnp.where(last_z, 0.0, pltpu.roll(value, 127, 1))
                slope[bit_x, bit_y] = after - value
                along[bit_x, bit_y] = value + z_weight * (after - value)
        for gauss_y in range(2):
            for gauss_x in range(2):
                point = 2 * gauss_x + gauss_y
                face = [lerp(along[bit_x, 0], along[bit_x, 1], gauss_y) for bit_x in range(2)]
                gradient[point, axis_id, 0] = face[1] - face[0]
                gradient[point, axis_id, 1] = lerp(
                    along[0, 1] - along[0, 0], along[1, 1] - along[1, 0], gauss_x
                )
                edge = [lerp(slope[bit_x, 0], slope[bit_x, 1], gauss_y) for bit_x in range(2)]
                gradient[point, axis_id, 2] = lerp(edge[0], edge[1], gauss_x)
    return [
        [
            gradient[point, 0, 0],
            gradient[point, 1, 1],
            gradient[point, 2, 2],
            gradient[point, 1, 2] + gradient[point, 2, 1],
            gradient[point, 0, 2] + gradient[point, 2, 0],
            gradient[point, 0, 1] + gradient[point, 1, 0],
        ]
        for point in range(4)
    ]


def weigh(low_value, high_value, corner_bit):
    if corner_bit:
        return LOW * low_value + HIGH * high_value
    return HIGH * low_value + LOW * high_value


def force_rows(stress):
    row = lax.broadcasted_iota(jnp.int32, (8, 128), 0)
    lane = lax.broadcasted_iota(jnp.int32, (8, 128), 1)
    z_high = jnp.where(row < 4, LOW, HIGH)
    z_low = jnp.where(row < 4, HIGH, LOW)
    voigt = [[0, 5, 4], [5, 1, 3], [4, 3, 2]]
    planes = [[None] * 3, [None] * 3]
    for axis_id in range(3):
        part = [[stress[point][voigt[axis_id][other]] for point in range(4)] for other in range(3)]
        flow = [part[0][gauss_y] + part[0][2 + gauss_y] for gauss_y in range(2)]
        for bit_x in range(2):
            side_y = [weigh(part[1][gauss_y], part[1][2 + gauss_y], bit_x) for gauss_y in range(2)]
            side_z = [weigh(part[2][gauss_y], part[2][2 + gauss_y], bit_x) for gauss_y in range(2)]
            total_y = side_y[0] + side_y[1]
            total = None
            for bit_y in range(2):
                first = weigh(flow[0], flow[1], bit_y)
                first = first if bit_x else -first
                first = first + total_y if bit_y else first - total_y
                second = weigh(side_z[0], side_z[1], bit_y)
                near = z_low * first - second
                far = z_high * first + second
                far = jnp.where(lane == 0, 0.0, pltpu.roll(far, 1, 1))
                both = near + far
                both = both + pltpu.roll(both, 4, 0)
                if bit_y:
                    both = jnp.where((row & 3) == 0, 0.0, pltpu.roll(both, 1, 0))
                total = both if total is None else total + both
            planes[bit_x][axis_id] = 0.125 * total
    return planes


def relax_kernel(
    near_ref,
    disp_ref,
    upper_ref,
    load_ref,
    tangent_ref,
    rank_ref,
    sel_ref,
    wt_ref,
    cd_ref,
    lp_ref,
    nrm_ref,
    nbr_ref,
    pre_ref,
    carried_ref,
    stress_ref,
    band_ref,
    dup_ref,
    strain_ref,
    split_high_ref,
    split_low_ref,
    affine_ref,
    fluct_ref,
    sums_ref,
    far_ref,
):
    tiles = strain_rows((disp_ref, upper_ref), dup_ref)
    for point in range(4):
        for comp in range(6):
            start = comp * 32 + point * 8
            strain_ref[start : start + 8, :] = tiles[point][comp]
    strain_ref[192:256, :] = jnp.zeros((64, 128), jnp.float32)

    for row in range(32):
        value = strain_ref[pl.ds(row, 8, stride=32), :]
        high = value.astype(jnp.bfloat16)
        split_high_ref[:, row * 128 : (row + 1) * 128] = high
        split_low_ref[:, row * 128 : (row + 1) * 128] = (value - high.astype(jnp.float32)).astype(
            jnp.bfloat16
        )
    sel = sel_ref[...]
    slot_strain = lax.dot_general(
        sel, split_high_ref[...], NT, preferred_element_type=jnp.float32
    ) + lax.dot_general(sel, split_low_ref[...], NT, preferred_element_type=jnp.float32)
    columns = [
        [
            jnp.broadcast_to(slot_strain[group * 8 : (group + 1) * 8, comp : comp + 1], (8, 128))
            for comp in range(6)
        ]
        for group in range(GROUPS)
    ]
    sums_ref[...] = jnp.zeros((192, 128), jnp.float32)

    def first_step(chunk, carry):
        lanes = lanes_of(chunk)
        totals = [[None] * 3 for _ in range(GROUPS)]
        for contact in range(CONTACTS):
            basis = [row8(lp_ref.at[comp], contact, lanes) for comp in range(6)]
            normal = [row8(nrm_ref.at[axis_id], contact, lanes) for axis_id in range(3)]
            for group in range(GROUPS):
                rows = slice(group * 8, (group + 1) * 8)
                affine = columns[group][0] * basis[0]
                for comp in range(1, 6):
                    affine = affine + columns[group][comp] * basis[comp]
                affine_ref[contact, rows, lanes] = affine
                force = wt_ref[contact, rows, lanes] * affine
                for axis_id in range(3):
                    term = force * normal[axis_id]
                    old = totals[group][axis_id]
                    totals[group][axis_id] = term if old is None else old + term
        for group in range(GROUPS):
            rows = slice(group * 8, (group + 1) * 8)
            factor = cd_ref[rows, lanes]
            for axis_id in range(3):
                start = axis_id * 32 + group * 8
                fluct_ref[0, start : start + 8, lanes] = factor * totals[group][axis_id]
        return carry

    lax.fori_loop(0, CHUNKS, first_step, 0)

    half = lax.broadcasted_iota(jnp.int32, (8, 128), 1) < 64

    def chunk_work(source, chunk, finish, near):
        lanes = lanes_of(chunk)
        lanes_up = lanes_of((chunk + 1) & (CHUNKS - 1))
        lanes_down = lanes_of((chunk + CHUNKS - 1) & (CHUNKS - 1))
        for group in range(GROUPS):
            rows = slice(group * 8, (group + 1) * 8)
            starts = [axis_id * 32 + group * 8 for axis_id in range(3)]
            own = [fluct_ref[source, start : start + 8, lanes] for start in starts]
            if near:
                sides = [
                    jnp.where(
                        half,
                        fluct_ref[source, start : start + 8, lanes_up],
                        fluct_ref[source, start : start + 8, lanes_down],
                    )
                    for start in starts
                ]
            stretches = []
            for contact in range(CONTACTS):
                normal = [row8(nrm_ref.at[axis_id], contact, lanes) for axis_id in range(3)]
                if near:
                    names = row8(nbr_ref, contact, lanes)
                    index = names & 127
                    inside = (names >> 7) == chunk
                    moved = [
                        jnp.where(
                            inside,
                            take_lanes(own[axis_id], index),
                            take_lanes(sides[axis_id], index),
                        )
                        for axis_id in range(3)
                    ]
                else:
                    moved = [far_ref[contact, start : start + 8, :] for start in starts]
                stretch = affine_ref[contact, rows, lanes]
                for axis_id in range(3):
                    stretch = stretch + normal[axis_id] * (moved[axis_id] - own[axis_id])
                force = wt_ref[contact, rows, lanes] * stretch
                stretches.append((force, normal))
            finish(group, rows, lanes, own, stretches)

    def gather_far(source, chunk):
        lanes = lanes_of(chunk)
        for contact in range(CONTACTS):
            names = row8(nbr_ref, contact, lanes)
            index = names & 127
            block = names >> 7

            def step(place, values):
                hit = block == place
                return tuple(
                    jnp.where(
                        hit,
                        take_lanes(
                            fluct_ref[source, tile * 8 : (tile + 1) * 8, lanes_of(place)], index
                        ),
                        values[tile],
                    )
                    for tile in range(12)
                )

            zero = jnp.zeros((8, 128), jnp.float32)
            values = lax.fori_loop(0, CHUNKS, step, (zero,) * 12)
            for tile in range(12):
                far_ref[contact, tile * 8 : (tile + 1) * 8, :] = values[tile]

    def both_ways(source, chunk, finish):
        near = near_ref[chunk] == 1

        @pl.when(near)
        def _():
            chunk_work(source, chunk, finish, True)

        @pl.when(jnp.logical_not(near))
        def _():
            gather_far(source, chunk)
            chunk_work(source, chunk, finish, False)

    def sweep_step(turn, carry):
        source = turn & 1
        target = 1 - source

        def finish(group, rows, lanes, own, stretches):
            factor = cd_ref[rows, lanes]
            for axis_id in range(3):
                total = None
                for force, normal in stretches:
                    term = force * normal[axis_id]
                    total = term if total is None else total + term
                start = axis_id * 32 + group * 8
                fluct_ref[target, start : start + 8, lanes] = own[axis_id] + factor * total

        def step(chunk, inner):
            both_ways(source, chunk, finish)
            return inner

        return lax.fori_loop(0, CHUNKS, step, carry)

    lax.fori_loop(0, SWEEPS - 1, sweep_step, 0)

    def finish_stress(group, rows, lanes, own, stretches):
        for comp in range(6):
            start = comp * 32 + group * 8
            total = sums_ref[start : start + 8, :]
            for contact in range(CONTACTS):
                total = total + stretches[contact][0] * row8(lp_ref.at[comp], contact, lanes)
            sums_ref[start : start + 8, :] = total

    def last_step(chunk, carry):
        both_ways((SWEEPS - 1) & 1, chunk, finish_stress)
        return carry

    lax.fori_loop(0, CHUNKS, last_step, 0)

    lane32 = lax.broadcasted_iota(jnp.int32, (32, 128), 1)
    table = jnp.zeros((32, 128), jnp.float32)
    for comp in range(6):
        total = jnp.sum(sums_ref[comp * 32 : (comp + 1) * 32, :], axis=1, keepdims=True)
        table = jnp.where(lane32 == comp, total * (1.0 / GRAINS), table)
    full = jnp.concatenate([table, jnp.zeros((96, 128), jnp.float32)], axis=0)
    flipped = jnp.transpose(full)
    band_ref[...] = flipped[0:6, 0:32]
    dup_ref[...] = flipped[0:8, :]

    strain = [strain_ref[comp * 32 : (comp + 1) * 32, :] for comp in range(6)]
    rank = rank_ref[...]
    banded = rank >= 0
    place = jnp.maximum(rank, 0)
    stress = []
    for row_id in range(6):
        running = None
        for col_id in range(6):
            where = PAIRS.index((min(row_id, col_id), max(row_id, col_id)))
            term = (
                tangent_ref[where * 32 : (where + 1) * 32, :].astype(jnp.float32) * strain[col_id]
            )
            running = term if running is None else running + term
        values = take_lanes(jnp.broadcast_to(dup_ref[row_id : row_id + 1, :], (32, 128)), place)
        value = jnp.where(banded, values, running)
        stress_ref[row_id * 32 : (row_id + 1) * 32, :] = value
        stress.append(value)
    planes = force_rows(
        [[stress[comp][point * 8 : (point + 1) * 8, :] for comp in range(6)] for point in range(4)]
    )
    for axis_id in range(3):
        pre_ref[axis_id] = load_ref[axis_id] - planes[0][axis_id][0:4]
        carried_ref[axis_id] = planes[1][axis_id][0:4]


VMEM = pl.BlockSpec(memory_space=pltpu.VMEM)
SMEM = pl.BlockSpec(memory_space=pltpu.SMEM)


def run_template(flags, stiffness, normals, branch_length, neighbours):
    f32 = jnp.float32
    return pl.pallas_call(
        template_kernel,
        out_shape=(
            jax.ShapeDtypeStruct((CONTACTS, SLOT_COUNT, GRAINS), f32),
            jax.ShapeDtypeStruct((SLOT_COUNT, GRAINS), f32),
            jax.ShapeDtypeStruct((21, SLOT_COUNT), f32),
            jax.ShapeDtypeStruct((32, 128), jnp.int32),
            jax.ShapeDtypeStruct((SLOT_COUNT, 4096), jnp.bfloat16),
            jax.ShapeDtypeStruct((6, CONTACTS, GRAINS), f32),
            jax.ShapeDtypeStruct((CHUNKS,), jnp.int32),
        ),
        in_specs=[VMEM] * 5,
        out_specs=(VMEM,) * 6 + (SMEM,),
        scratch_shapes=[
            pltpu.VMEM((SLOT_COUNT * CONTACTS, 128), f32),
            pltpu.VMEM((256, 128), f32),
            pltpu.VMEM((CONTACTS, 32, GRAINS), jnp.bfloat16),
            pltpu.VMEM((CONTACTS, 32, GRAINS), jnp.bfloat16),
        ],
        cost_estimate=pl.CostEstimate(flops=40_000_000, bytes_accessed=8_000_000, transcendentals=0),
        name="template",
    )(flags, stiffness, normals, branch_length, neighbours)


def run_relax(near, disp, upper, load, tangent, rank, sel, wt, cd, lp, normals, neighbours):
    f32 = jnp.float32
    return pl.pallas_call(
        relax_kernel,
        out_shape=(
            jax.ShapeDtypeStruct((3, 4, 128), f32),
            jax.ShapeDtypeStruct((3, 4, 128), f32),
            jax.ShapeDtypeStruct((192, 128), f32),
            jax.ShapeDtypeStruct((6, SLOT_COUNT), f32),
        ),
        in_specs=[SMEM] + [VMEM] * 11,
        out_specs=(VMEM,) * 4,
        scratch_shapes=[
            pltpu.VMEM((8, 128), f32),
            pltpu.VMEM((256, 128), f32),
            pltpu.VMEM((8, 4096), jnp.bfloat16),
            pltpu.VMEM((8, 4096), jnp.bfloat16),
            pltpu.VMEM((CONTACTS, SLOT_COUNT, GRAINS), f32),
            pltpu.VMEM((2, 96, GRAINS), f32),
            pltpu.VMEM((192, 128), f32),
            pltpu.VMEM((CONTACTS, 96, 128), f32),
        ],
        cost_estimate=pl.CostEstimate(
            flops=200_000_000, bytes_accessed=8_000_000, transcendentals=0
        ),
        name="relax",
    )(near, disp, upper, load, tangent, rank, sel, wt, cd, lp, normals, neighbours)


def body(
    displacement,
    load,
    elastic_tangent,
    band_flags,
    contact_stiffness,
    normals,
    branch_length,
    neighbours,
):
    upper = shifted(displacement, ("row", "col"), -1)
    wt, cd, tangent, rank, sel, lp, near = run_template(
        band_flags.reshape(32, 128), contact_stiffness, normals, branch_length, neighbours
    )
    pre, carried, stress, band = run_relax(
        near,
        displacement.reshape(3, 4, 128),
        upper.reshape(3, 4, 128),
        load.reshape(3, 4, 128),
        elastic_tangent.reshape(672, 128),
        rank,
        sel,
        wt,
        cd,
        lp,
        normals,
        neighbours,
    )
    arrived = shifted(carried, ("row", "col"), 1)
    residual = (pre - arrived).reshape(3, 1, 4, 128)
    return (residual, stress.reshape(6, 8, 1, 4, 128), tangent, band)


def solution(mesh):
    placed = (
        P(None, ("row", "col"), None, None),
        P(None, ("row", "col"), None, None),
        P(None, None, ("row", "col"), None, None),
        P(None, ("row", "col"), None, None),
        P(("row", "col"), None, None),
        P(),
        P(),
        P(),
    )
    return jax.shard_map(
        body,
        mesh=mesh,
        in_specs=placed,
        out_specs=(
            P(None, ("row", "col"), None, None),
            P(None, None, ("row", "col"), None, None),
            P(None, ("row", "col")),
            P(None, ("row", "col")),
        ),
        check_vma=False,
    )
```

time: 2190 us -> 67.6 us (0.03)
  local copies, waits for them, and re-layouts: 1300 us -> 0.59 us
  starting transfers between devices: 735 us -> 8.01 us
  other arithmetic: 54.6 us -> 1.29 us
  Pallas kernels: 0 us -> 48.1 us
  matrix products: 46 us -> 0 us
  waiting for transfers between devices: 41.1 us -> 8.66 us
    gather x28 -> x0, local copies, waits for them, and re-layouts: 1240 us -> none  [the longest x18 1230 us: relax_rve(): fluctuation[:, neighbours] - fluctuation[:, None, :]]
    all_to_all x5 -> x0, starting transfers between devices: 727 us -> none  [the longest x1 690 us: body(): lax.all_to_all(out_stress.reshape(sources, items, 6), 'row', split_axis=0...]
    pallas_call x0 -> x2, Pallas kernels: none -> 48.1 us  [the longest x1 43.5 us: run_relax(): pl.pallas_call(relax_kernel, out_shape=(jax.ShapeDtypeStruct((3, 4, 128),...]
    dot_general x8 -> x0, matrix products: 46 us -> none  [the longest x2 41.4 us: relax_rve(): jnp.dot(flat_proj * stiff_term[None, :], flat_proj.T, precision=lax.Preci...]
    reduce_sum x23 -> x0, other arithmetic: 36.2 us -> none  [the longest x10 29.5 us: relax_rve(): jnp.sum(normals * (fluctuation[:, neighbours] - fluctuation[:, None, :]),...]
    all_to_all x5 -> x0, waiting for transfers between devices: 34 us -> none  [the longest x1 30.8 us: body(): lax.all_to_all(stiff_send, 'row', split_axis=0, concat_axis=0, tiled=True)]
    add x15 -> x0, local copies, waits for them, and re-layouts: 21.9 us -> none  [the longest x6 18.3 us: relax_rve(): fluctuation = fluctuation + RELAX_FACTOR * unbalanced / diagonal[None, :]]
  transfers between devices with their start and end apart: 7 -> 2, of which waited for: 3 -> 1; matrix products, arithmetic and copies ran while one was open for 2% -> 0% of each run, Pallas kernels for 0% -> 7%
where the time goes in v1:
time: 67.6 us; the launch traced here: 67.4 us
  Pallas kernels  48.1 us (71%)
  waiting for transfers between devices  8.66 us (13%)
  starting transfers between devices  8.01 us (12%)
  other arithmetic  1.29 us (2%)
    pallas_call x1, Pallas kernels, run_relax(): pl.pallas_call(relax_kernel, out_shape=(jax.ShapeDtypeStruct((3, 4, 128),...  43.5 us
    ppermute x2, waiting for transfers between devices, shifted(): lax.ppermute(value, axis, [(source, source + steps) for source in range(l...  8.66 us
    ppermute x2, starting transfers between devices, shifted(): lax.ppermute(value, axis, [(source, source + steps) for source in range(l...  8.01 us
    pallas_call x1, Pallas kernels, run_template(): pl.pallas_call(template_kernel, out_shape=(jax.ShapeDtypeStruct((CONTACTS...  4.68 us
  transfers between devices with their start and end apart: 2, of which 1 were waited for; matrix products, arithmetic and copies ran while one was open for 0% of the time, Pallas kernels for 7%

profile of v1, /device:TPU:128, one launch (start us, length us, event | category | flops | bytes accessed | tf_op | source)
XLA Modules:
  0.0 67.4 jit_solution(5540164230382144462)
XLA Ops:
  0.6 6.1 %collective-permute-start = (f32[3,1,4,128]{3,2,0,1:T(4,128)}, f32[3,1,4,128]{3,2,0,1:T(4,128)S(1)}, u32[]{:S(2)}, u32[]{:S(2)}) collective-permute-start(f32[3,1,4,128]{3,2,0,1:T(4,128)} %bitcast.15), channel_id=1, source_target_pairs={{1,0},{2,1},{3,2},{4,3},{5,4},{6,5},{7,6},{8,7},{9,8},{10,9},{11,1... | collective-permute-start | bytes 18440 | tf_op jit(solution)/shard_map/ppermute | solution.py:25
  6.7 4.7 %template.1 = (f32[8,32,2048]{2,1,0:T(8,128)}, f32[32,2048]{1,0:T(8,128)}, f32[21,32]{1,0:T(8,128)}, s32[32,128]{1,0:T(8,128)}, bf16[32,4096]{1,0:T(8,128)(2,1)}, /*index=5*/f32[6,8,2048]{2,1,0:T(8,128)}, s32[16]{0:T(128)}) custom-call(s32[32,128]{1,0:T(8,128)} %bitcast.14, bf16[32,8,2048]{2,1,0:T(8,128)(2,1)} %stiff_ref.1, f32[3,8,2048]{2,1,0:T(8,128)} %nrm_ref.3, ...), custom_call_target="tpu_custom_call" | custom-call | flops 40000000 | bytes 8000000 | tf_op jit(solution)/shard_map/template/pallas_call | solution.py:455
  11.4 0.0 collective-permute-done
  11.4 0.0 copy-start
  11.4 0.6 copy-done
  12.0 43.5 %relax.1 = (f32[3,4,128]{2,1,0:T(4,128)}, f32[3,4,128]{2,1,0:T(4,128)}, f32[192,128]{1,0:T(8,128)}, f32[6,32]{1,0:T(8,128)}) custom-call(s32[16]{0:T(128)} %get-tuple-element.15.near_ref, f32[3,4,128]{2,1,0:T(4,128)} %bitcast.16, f32[3,4,128]{2,1,0:T(4,128)} %bitcast.18, f32[3,4,128]{2,1,0:T(4,128)} %bitcast.17, bf16[672,128]{1,0:T(8,128)(2,1)} %bitcast.13, ...), custom_call_target="tpu_custom_call" | custom-call | flops 200000000 | bytes 8000000 | tf_op jit(solution)/shard_map/relax/pallas_call | solution.py:481
  55.5 1.9 %collective-permute-start.1 = (f32[3,4,128]{2,1,0:T(4,128)}, f32[3,4,128]{2,1,0:T(4,128)S(1)}, u32[]{:S(2)}, u32[]{:S(2)}) collective-permute-start(f32[3,4,128]{2,1,0:T(4,128)} %get-tuple-element.22), channel_id=1, source_target_pairs={{0,1},{1,2},{2,3},{3,4},{4,5},{5,6},{6,7},{7,8},{8,9},{9,10},{10,1... | collective-permute-start | bytes 18440 | tf_op jit(solution)/shard_map/ppermute | solution.py:25
  57.4 8.7 %collective-permute-done.1 = f32[3,4,128]{2,1,0:T(4,128)S(1)} collective-permute-done((f32[3,4,128]{2,1,0:T(4,128)}, f32[3,4,128]{2,1,0:T(4,128)S(1)}, u32[]{:S(2)}, u32[]{:S(2)}) %collective-permute-start.1) | collective-permute-done | bytes 6176 | tf_op jit(solution)/shard_map/ppermute | solution.py:25
  66.1 1.3 %subtract_bitcast_fusion = f32[3,1,4,128]{3,2,1,0:T(4,128)} fusion(f32[3,4,128]{2,1,0:T(4,128)} %get-tuple-element.21, f32[3,4,128]{2,1,0:T(4,128)S(1)} %collective-permute-done.1), kind=kLoop, calls=%fused_computation | loop fusion | flops 1536 | bytes 18432
Async XLA Ops:
  0.6 10.8 %collective-permute-start = (f32[3,1,4,128]{3,2,0,1:T(4,128)}, f32[3,1,4,128]{3,2,0,1:T(4,128)S(1)}, u32[]{:S(2)}, u32[]{:S(2)}) collective-permute-start(f32[3,1,4,128]{3,2,0,1:T(4,128)} %bitcast.15), channel_id=1, source_target_pairs={{1,0},{2,1},{3,2},{4,3},{5,4},{6,5},{7,6},{8,7},{9,8},{10,9},{11,1... | collective-permute-start | bytes 18440 | tf_op jit(solution)/shard_map/ppermute | solution.py:25
  11.4 0.6 copy-start
  55.5 10.6 %collective-permute-start.1 = (f32[3,4,128]{2,1,0:T(4,128)}, f32[3,4,128]{2,1,0:T(4,128)S(1)}, u32[]{:S(2)}, u32[]{:S(2)}) collective-permute-start(f32[3,4,128]{2,1,0:T(4,128)} %get-tuple-element.22), channel_id=1, source_target_pairs={{0,1},{1,2},{2,3},{3,4},{4,5},{5,6},{6,7},{7,8},{8,9},{9,10},{10,1... | collective-permute-start | bytes 18440 | tf_op jit(solution)/shard_map/ppermute | solution.py:25

commit v2 on v1

--- a/solution.py
+++ b/solution.py
@@ -15,6 +15,7 @@
 SLOT_COUNT = 32
 GROUPS = SLOT_COUNT // 8
 CHUNKS = GRAINS // 128
+UNROLL = 4
 PAIRS = [(row_id, col_id) for row_id in range(6) for col_id in range(row_id, 6)]
 NT = (((1,), (1,)), ((), ()))
 
@@ -33,8 +34,23 @@
     return jnp.broadcast_to(ref[row : row + 1, lanes], (8, 128))
 
 
+LANE_GATHER = lax.GatherDimensionNumbers(
+    offset_dims=(),
+    collapsed_slice_dims=(1,),
+    start_index_map=(1,),
+    operand_batching_dims=(0,),
+    start_indices_batching_dims=(0,),
+)
+
+
 def take_lanes(table, index):
-    return jnp.take_along_axis(table, index, axis=1, mode="promise_in_bounds")
+    return lax.gather(
+        table,
+        index[..., None],
+        LANE_GATHER,
+        slice_sizes=(1, 1),
+        mode=lax.GatherScatterMode.PROMISE_IN_BOUNDS,
+    )
 
 
 def template_kernel(
@@ -49,7 +65,6 @@
     rank_ref,
     sel_ref,
     lp_ref,
-    near_ref,
     raw_ref,
     basis_ref,
     high_ref,
@@ -77,13 +92,6 @@
         sel_ref[:, row * 128 : (row + 1) * 128] = jnp.where(picked, 1.0, 0.0).astype(jnp.bfloat16)
 
     basis_ref[168:256, :] = jnp.zeros((88, 128), jnp.float32)
-    for chunk in range(CHUNKS):
-        lanes = slice(chunk * 128, (chunk + 1) * 128)
-        names = nbr_ref[:, lanes]
-        own = lax.broadcasted_iota(jnp.int32, (8, 128), 1) + chunk * 128
-        reach = (names - (chunk * 128 - 64)) & (GRAINS - 1)
-        widest = jnp.max(reach.astype(jnp.float32))
-        near_ref[chunk] = (widest < 256.0).astype(jnp.int32)
 
     def chunk_step(chunk, carry):
         lanes = lanes_of(chunk)
@@ -216,7 +224,6 @@
 
 
 def relax_kernel(
-    near_ref,
     disp_ref,
     upper_ref,
     load_ref,
@@ -228,6 +235,7 @@
     lp_ref,
     nrm_ref,
     nbr_ref,
+    tan_ref,
     pre_ref,
     carried_ref,
     stress_ref,
@@ -236,11 +244,23 @@
     strain_ref,
     split_high_ref,
     split_low_ref,
-    affine_ref,
-    fluct_ref,
+    first_ref,
+    fluct_a_ref,
+    fluct_b_ref,
     sums_ref,
-    far_ref,
+    onehot_ref,
+    moved_ref,
+    names_ref,
+    near_ref,
 ):
+    near_total = 0
+    for chunk in range(CHUNKS):
+        reach = (nbr_ref[:, chunk * 128 : (chunk + 1) * 128] - (chunk * 128 - 64)) & (GRAINS - 1)
+        near_one = (jnp.max(reach.astype(jnp.float32)) < 256.0).astype(jnp.int32)
+        near_ref[chunk] = near_one
+        near_total = near_total + near_one
+    all_near = near_total == CHUNKS
+
     tiles = strain_rows((disp_ref, upper_ref), dup_ref)
     for point in range(4):
         for comp in range(6):
@@ -266,82 +286,122 @@
         ]
         for group in range(GROUPS)
     ]
+    strain_t = lax.dot_general(
+        split_high_ref[...], sel, NT, preferred_element_type=jnp.float32
+    ) + lax.dot_general(split_low_ref[...], sel, NT, preferred_element_type=jnp.float32)
     sums_ref[...] = jnp.zeros((192, 128), jnp.float32)
 
     def first_step(chunk, carry):
         lanes = lanes_of(chunk)
-        totals = [[None] * 3 for _ in range(GROUPS)]
+        block = lax.broadcasted_iota(jnp.int32, (16, 128), 0).astype(jnp.float32)
         for contact in range(CONTACTS):
-            basis = [row8(lp_ref.at[comp], contact, lanes) for comp in range(6)]
-            normal = [row8(nrm_ref.at[axis_id], contact, lanes) for axis_id in range(3)]
-            for group in range(GROUPS):
-                rows = slice(group * 8, (group + 1) * 8)
-                affine = columns[group][0] * basis[0]
-                for comp in range(1, 6):
-                    affine = affine + columns[group][comp] * basis[comp]
-                affine_ref[contact, rows, lanes] = affine
-                force = wt_ref[contact, rows, lanes] * affine
+            names = jnp.broadcast_to(nbr_ref[contact : contact + 1, lanes], (16, 128))
+            wanted = (names & 127) + jnp.where((names >> 7) == chunk, 0, 128)
+            wanted = (wanted.astype(jnp.float32) - block).astype(jnp.bfloat16)
+            onehot_ref[chunk * CONTACTS + contact] = jnp.concatenate(
+                [
+                    jnp.where(wanted == jnp.bfloat16(part * 16), jnp.bfloat16(1), jnp.bfloat16(0))
+                    for part in range(16)
+                ],
+                axis=0,
+            )
+        for pair in range(0, GROUPS, 2):
+            groups = (pair, pair + 1)
+            totals = {}
+            for contact in range(CONTACTS):
+                basis = [row8(lp_ref.at[comp], contact, lanes) for comp in range(6)]
+                normal = [row8(nrm_ref.at[axis_id], contact, lanes) for axis_id in range(3)]
+                for group in groups:
+                    rows = slice(group * 8, (group + 1) * 8)
+                    affine = columns[group][0] * basis[0]
+                    for comp in range(1, 6):
+                        affine = affine + columns[group][comp] * basis[comp]
+                    force = wt_ref[contact, rows, lanes] * affine
+                    for axis_id in range(3):
+                        term = force * normal[axis_id]
+                        key = (group, axis_id)
+                        totals[key] = totals[key] + term if contact else term
+            for group in groups:
+                factor = cd_ref[group * 8 : (group + 1) * 8, lanes]
                 for axis_id in range(3):
-                    term = force * normal[axis_id]
-                    old = totals[group][axis_id]
-                    totals[group][axis_id] = term if old is None else old + term
-        for group in range(GROUPS):
-            rows = slice(group * 8, (group + 1) * 8)
-            factor = cd_ref[rows, lanes]
-            for axis_id in range(3):
-                start = axis_id * 32 + group * 8
-                fluct_ref[0, start : start + 8, lanes] = factor * totals[group][axis_id]
+                    start = axis_id * 32 + group * 8
+                    first_ref[start : start + 8, lanes] = factor * totals[group, axis_id]
         return carry
 
     lax.fori_loop(0, CHUNKS, first_step, 0)
 
     half = lax.broadcasted_iota(jnp.int32, (8, 128), 1) < 64
 
-    def chunk_work(source, chunk, finish, near):
+    def gather_near(source_ref, chunk, moved_ref):
         lanes = lanes_of(chunk)
         lanes_up = lanes_of((chunk + 1) & (CHUNKS - 1))
         lanes_down = lanes_of((chunk + CHUNKS - 1) & (CHUNKS - 1))
-        for group in range(GROUPS):
-            rows = slice(group * 8, (group + 1) * 8)
-            starts = [axis_id * 32 + group * 8 for axis_id in range(3)]
-            own = [fluct_ref[source, start : start + 8, lanes] for start in starts]
-            if near:
-                sides = [
-                    jnp.where(
-                        half,
-                        fluct_ref[source, start : start + 8, lanes_up],
-                        fluct_ref[source, start : start + 8, lanes_down],
-                    )
-                    for start in starts
-                ]
-            stretches = []
-            for contact in range(CONTACTS):
+        tiles = [slice(tile * 8, (tile + 1) * 8) for tile in range(12)]
+        own = [source_ref[tile, lanes] for tile in tiles]
+        sides = [
+            jnp.where(half, source_ref[tile, lanes_up], source_ref[tile, lanes_down])
+            for tile in tiles
+        ]
+        for contact in range(CONTACTS):
+            names = row8(nbr_ref, contact, lanes)
+            index = names & 127
+            inside = (names >> 7) == chunk
+            for place, tile in enumerate(tiles):
+                moved_ref[tile, contact * 128 : (contact + 1) * 128] = jnp.where(
+                    inside, take_lanes(own[place], index), take_lanes(sides[place], index)
+                )
+
+    tall = lax.broadcasted_iota(jnp.int32, (96, 128), 1) < 64
+
+    def dot_pieces(source_ref, chunk):
+        lanes = lanes_of(chunk)
+        lanes_up = lanes_of((chunk + 1) & (CHUNKS - 1))
+        lanes_down = lanes_of((chunk + CHUNKS - 1) & (CHUNKS - 1))
+        own = source_ref[:, lanes]
+        sides = jnp.where(tall, source_ref[:, lanes_up], source_ref[:, lanes_down])
+        window = jnp.concatenate([own, sides], axis=1)
+        high = window.astype(jnp.bfloat16)
+        low = (window - high.astype(jnp.float32)).astype(jnp.bfloat16)
+        both = jnp.concatenate([high, low], axis=0)
+
+        def pieces(pair):
+            place = chunk * CONTACTS + 2 * pair
+            picks = jnp.concatenate([onehot_ref[place], onehot_ref[place + 1]], axis=1)
+            value = jnp.dot(both, picks, preferred_element_type=jnp.float32)
+            return value[0:96] + value[96:192]
+
+        return pieces
+
+    def scratch_pieces(moved_ref):
+        return lambda pair: moved_ref[:, pair * 256 : (pair + 1) * 256]
+
+    def chunk_forces(source_ref, chunk, pieces, use):
+        lanes = lanes_of(chunk)
+        own = [source_ref[tile * 8 : (tile + 1) * 8, lanes] for tile in range(12)]
+        for pair in range(CONTACTS // 2):
+            moved = pieces(pair)
+            for half_id in range(2):
+                contact = 2 * pair + half_id
+                columns_of = slice(half_id * 128, (half_id + 1) * 128)
                 normal = [row8(nrm_ref.at[axis_id], contact, lanes) for axis_id in range(3)]
-                if near:
-                    names = row8(nbr_ref, contact, lanes)
-                    index = names & 127
-                    inside = (names >> 7) == chunk
-                    moved = [
-                        jnp.where(
-                            inside,
-                            take_lanes(own[axis_id], index),
-                            take_lanes(sides[axis_id], index),
-                        )
-                        for axis_id in range(3)
-                    ]
-                else:
-                    moved = [far_ref[contact, start : start + 8, :] for start in starts]
-                stretch = affine_ref[contact, rows, lanes]
-                for axis_id in range(3):
-                    stretch = stretch + normal[axis_id] * (moved[axis_id] - own[axis_id])
-                force = wt_ref[contact, rows, lanes] * stretch
-                stretches.append((force, normal))
-            finish(group, rows, lanes, own, stretches)
-
-    def gather_far(source, chunk):
+                for group in range(GROUPS):
+                    stretch = None
+                    for axis_id in range(3):
+                        tile = axis_id * 4 + group
+                        there = moved[tile * 8 : (tile + 1) * 8, columns_of]
+                        term = normal[axis_id] * (there - own[tile])
+                        stretch = term if stretch is None else stretch + term
+                    rows = slice(group * 8, (group + 1) * 8)
+                    use(contact, group, wt_ref[contact, rows, lanes] * stretch, normal)
+        return own
+
+    def gather_far(source_ref, chunk, moved_ref):
         lanes = lanes_of(chunk)
         for contact in range(CONTACTS):
-            names = row8(nbr_ref, contact, lanes)
+            names_ref[contact] = row8(nbr_ref, contact, lanes)
+
+        def contact_step(contact, carry):
+            names = names_ref[contact]
             index = names & 127
             block = names >> 7
 
@@ -350,9 +410,7 @@
                 return tuple(
                     jnp.where(
                         hit,
-                        take_lanes(
-                            fluct_ref[source, tile * 8 : (tile + 1) * 8, lanes_of(place)], index
-                        ),
+                        take_lanes(source_ref[tile * 8 : (tile + 1) * 8, lanes_of(place)], index),
                         values[tile],
                     )
                     for tile in range(12)
@@ -361,55 +419,81 @@
             zero = jnp.zeros((8, 128), jnp.float32)
             values = lax.fori_loop(0, CHUNKS, step, (zero,) * 12)
             for tile in range(12):
-                far_ref[contact, tile * 8 : (tile + 1) * 8, :] = values[tile]
-
-    def both_ways(source, chunk, finish):
-        near = near_ref[chunk] == 1
-
-        @pl.when(near)
+                moved_ref[tile * 8 : (tile + 1) * 8, lanes_of(contact)] = values[tile]
+            return carry
+
+        lax.fori_loop(0, CONTACTS, contact_step, 0)
+
+    def all_chunks(source_ref, work):
+        @pl.when(all_near)
         def _():
-            chunk_work(source, chunk, finish, True)
-
-        @pl.when(jnp.logical_not(near))
+            def step(turn, carry):
+                for place in range(UNROLL):
+                    chunk = turn * UNROLL + place
+                    work(chunk, dot_pieces(source_ref, chunk))
+                return carry
+
+            lax.fori_loop(0, CHUNKS // UNROLL, step, 0)
+
+        @pl.when(jnp.logical_not(all_near))
         def _():
-            gather_far(source, chunk)
-            chunk_work(source, chunk, finish, False)
-
-    def sweep_step(turn, carry):
-        source = turn & 1
-        target = 1 - source
-
-        def finish(group, rows, lanes, own, stretches):
-            factor = cd_ref[rows, lanes]
-            for axis_id in range(3):
-                total = None
-                for force, normal in stretches:
+            def step(chunk, carry):
+                near = near_ref[chunk] == 1
+
+                @pl.when(near)
+                def _():
+                    gather_near(source_ref, chunk, moved_ref)
+
+                @pl.when(jnp.logical_not(near))
+                def _():
+                    gather_far(source_ref, chunk, moved_ref)
+
+                work(chunk, scratch_pieces(moved_ref))
+                return carry
+
+            lax.fori_loop(0, CHUNKS, step, 0)
+
+    def sweep(source_ref, target_ref):
+        def work(chunk, pieces):
+            totals = [None] * 12
+
+            def use(contact, group, force, normal):
+                for axis_id in range(3):
+                    tile = axis_id * 4 + group
                     term = force * normal[axis_id]
-                    total = term if total is None else total + term
-                start = axis_id * 32 + group * 8
-                fluct_ref[target, start : start + 8, lanes] = own[axis_id] + factor * total
-
-        def step(chunk, inner):
-            both_ways(source, chunk, finish)
-            return inner
-
-        return lax.fori_loop(0, CHUNKS, step, carry)
-
-    lax.fori_loop(0, SWEEPS - 1, sweep_step, 0)
-
-    def finish_stress(group, rows, lanes, own, stretches):
-        for comp in range(6):
-            start = comp * 32 + group * 8
-            total = sums_ref[start : start + 8, :]
-            for contact in range(CONTACTS):
-                total = total + stretches[contact][0] * row8(lp_ref.at[comp], contact, lanes)
-            sums_ref[start : start + 8, :] = total
-
-    def last_step(chunk, carry):
-        both_ways((SWEEPS - 1) & 1, chunk, finish_stress)
-        return carry
-
-    lax.fori_loop(0, CHUNKS, last_step, 0)
+                    totals[tile] = totals[tile] + term if contact else term
+
+            own = chunk_forces(source_ref, chunk, pieces, use)
+            lanes = lanes_of(chunk)
+            for group in range(GROUPS):
+                factor = cd_ref[group * 8 : (group + 1) * 8, lanes]
+                for axis_id in range(3):
+                    tile = axis_id * 4 + group
+                    rows = slice(tile * 8, (tile + 1) * 8)
+                    target_ref[rows, lanes] = own[tile] + first_ref[rows, lanes] + factor * totals[tile]
+
+        all_chunks(source_ref, work)
+
+    def stress_work(chunk, pieces):
+        lanes = lanes_of(chunk)
+        totals = [None] * 24
+
+        def use(contact, group, force, normal):
+            for comp in range(6):
+                tile = comp * 4 + group
+                term = force * row8(lp_ref.at[comp], contact, lanes)
+                totals[tile] = totals[tile] + term if contact else term
+
+        chunk_forces(current, chunk, pieces, use)
+        for tile in range(24):
+            sums_ref[tile * 8 : (tile + 1) * 8, :] += totals[tile]
+
+    current = first_ref
+    for turn in range(SWEEPS - 1):
+        target = fluct_b_ref if turn % 2 else fluct_a_ref
+        sweep(current, target)
+        current = target
+    all_chunks(current, stress_work)
 
     lane32 = lax.broadcasted_iota(jnp.int32, (32, 128), 1)
     table = jnp.zeros((32, 128), jnp.float32)
@@ -417,9 +501,17 @@
         total = jnp.sum(sums_ref[comp * 32 : (comp + 1) * 32, :], axis=1, keepdims=True)
         table = jnp.where(lane32 == comp, total * (1.0 / GRAINS), table)
     full = jnp.concatenate([table, jnp.zeros((96, 128), jnp.float32)], axis=0)
-    flipped = jnp.transpose(full)
-    band_ref[...] = flipped[0:6, 0:32]
-    dup_ref[...] = flipped[0:8, :]
+    shares = []
+    for row_id in range(6):
+        share = None
+        for col_id in range(6):
+            where = PAIRS.index((min(row_id, col_id), max(row_id, col_id)))
+            term = tan_ref[where : where + 1, :] * strain_t[col_id : col_id + 1, :]
+            share = term if share is None else share + term
+        shares.append(share)
+    flipped = jnp.transpose(full)[0:6, 0:32] + jnp.concatenate(shares, axis=0)
+    band_ref[...] = flipped
+    dup_ref[0:6, 0:32] = flipped
 
     strain = [strain_ref[comp * 32 : (comp + 1) * 32, :] for comp in range(6)]
     rank = rank_ref[...]
@@ -447,7 +539,6 @@
 
 
 VMEM = pl.BlockSpec(memory_space=pltpu.VMEM)
-SMEM = pl.BlockSpec(memory_space=pltpu.SMEM)
 
 
 def run_template(flags, stiffness, normals, branch_length, neighbours):
@@ -461,10 +552,9 @@
             jax.ShapeDtypeStruct((32, 128), jnp.int32),
             jax.ShapeDtypeStruct((SLOT_COUNT, 4096), jnp.bfloat16),
             jax.ShapeDtypeStruct((6, CONTACTS, GRAINS), f32),
-            jax.ShapeDtypeStruct((CHUNKS,), jnp.int32),
         ),
         in_specs=[VMEM] * 5,
-        out_specs=(VMEM,) * 6 + (SMEM,),
+        out_specs=(VMEM,) * 6,
         scratch_shapes=[
             pltpu.VMEM((SLOT_COUNT * CONTACTS, 128), f32),
             pltpu.VMEM((256, 128), f32),
@@ -476,7 +566,7 @@
     )(flags, stiffness, normals, branch_length, neighbours)
 
 
-def run_relax(near, disp, upper, load, tangent, rank, sel, wt, cd, lp, normals, neighbours):
+def run_relax(disp, upper, load, tangent, rank, sel, wt, cd, lp, normals, neighbours, tan):
     f32 = jnp.float32
     return pl.pallas_call(
         relax_kernel,
@@ -486,23 +576,27 @@
             jax.ShapeDtypeStruct((192, 128), f32),
             jax.ShapeDtypeStruct((6, SLOT_COUNT), f32),
         ),
-        in_specs=[SMEM] + [VMEM] * 11,
+        in_specs=[VMEM] * 12,
         out_specs=(VMEM,) * 4,
         scratch_shapes=[
             pltpu.VMEM((8, 128), f32),
             pltpu.VMEM((256, 128), f32),
             pltpu.VMEM((8, 4096), jnp.bfloat16),
             pltpu.VMEM((8, 4096), jnp.bfloat16),
-            pltpu.VMEM((CONTACTS, SLOT_COUNT, GRAINS), f32),
-            pltpu.VMEM((2, 96, GRAINS), f32),
+            pltpu.VMEM((96, GRAINS), f32),
+            pltpu.VMEM((96, GRAINS), f32),
+            pltpu.VMEM((96, GRAINS), f32),
             pltpu.VMEM((192, 128), f32),
-            pltpu.VMEM((CONTACTS, 96, 128), f32),
+            pltpu.VMEM((CHUNKS * CONTACTS, 256, 128), jnp.bfloat16),
+            pltpu.VMEM((96, CONTACTS * 128), f32),
+            pltpu.VMEM((CONTACTS, 8, 128), jnp.int32),
+            pltpu.SMEM((CHUNKS,), jnp.int32),
         ],
         cost_estimate=pl.CostEstimate(
             flops=200_000_000, bytes_accessed=8_000_000, transcendentals=0
         ),
         name="relax",
-    )(near, disp, upper, load, tangent, rank, sel, wt, cd, lp, normals, neighbours)
+    )(disp, upper, load, tangent, rank, sel, wt, cd, lp, normals, neighbours, tan)
 
 
 def body(
@@ -516,11 +610,10 @@
     neighbours,
 ):
     upper = shifted(displacement, ("row", "col"), -1)
-    wt, cd, tangent, rank, sel, lp, near = run_template(
+    wt, cd, tangent, rank, sel, lp = run_template(
         band_flags.reshape(32, 128), contact_stiffness, normals, branch_length, neighbours
     )
     pre, carried, stress, band = run_relax(
-        near,
         displacement.reshape(3, 4, 128),
         upper.reshape(3, 4, 128),
         load.reshape(3, 4, 128),
@@ -532,6 +625,7 @@
         lp,
         normals,
         neighbours,
+        tangent,
     )
     arrived = shifted(carried, ("row", "col"), 1)
     residual = (pre - arrived).reshape(3, 1, 4, 128)

time: 67.6 us -> 42.1 us (0.62)
  Pallas kernels: 48.1 us -> 22.7 us
    pallas_call x1, Pallas kernels: 43.5 us -> 18 us  [run_relax(): pl.pallas_call(relax_kernel, out_shape=(jax.ShapeDtypeStruct((3, 4, 128),...]
  transfers between devices with their start and end apart: 2 -> 2, of which waited for: 1 -> 1; matrix products, arithmetic and copies ran while one was open for 0% -> 0% of each run, Pallas kernels for 7% -> 11%
where the time goes in v2:
time: 42.1 us; the launch traced here: 41.9 us
  Pallas kernels  22.7 us (54%)
  waiting for transfers between devices  8.66 us (21%)
  starting transfers between devices  8.01 us (19%)
  other arithmetic  1.29 us (3%)
  between operations  0.65 us (2%)
  local copies, waits for them, and re-layouts  0.59 us (1%)
    pallas_call x1, Pallas kernels, run_relax(): pl.pallas_call(relax_kernel, out_shape=(jax.ShapeDtypeStruct((3, 4, 128),...  18 us
    ppermute x2, waiting for transfers between devices, shifted(): lax.ppermute(value, axis, [(source, source + steps) for source in range(l...  8.66 us
    ppermute x2, starting transfers between devices, shifted(): lax.ppermute(value, axis, [(source, source + steps) for source in range(l...  8.01 us
    pallas_call x1, Pallas kernels, run_template(): pl.pallas_call(template_kernel, out_shape=(jax.ShapeDtypeStruct((CONTACTS...  4.66 us
    unnamed x1, other arithmetic  1.29 us
  transfers between devices with their start and end apart: 2, of which 1 were waited for; matrix products, arithmetic and copies ran while one was open for 0% of the time, Pallas kernels for 11%

profile of v2, /device:TPU:128, one launch (start us, length us, event | category | flops | bytes accessed | tf_op | source)
XLA Modules:
  0.0 41.9 jit_solution(3274724122339964530)
XLA Ops:
  0.6 6.1 %collective-permute-start = (f32[3,1,4,128]{3,2,0,1:T(4,128)}, f32[3,1,4,128]{3,2,0,1:T(4,128)S(1)}, u32[]{:S(2)}, u32[]{:S(2)}) collective-permute-start(f32[3,1,4,128]{3,2,0,1:T(4,128)} %bitcast.15), channel_id=1, source_target_pairs={{1,0},{2,1},{3,2},{4,3},{5,4},{6,5},{7,6},{8,7},{9,8},{10,9},{11,1... | collective-permute-start | bytes 18440 | tf_op jit(solution)/shard_map/ppermute | solution.py:26
  6.7 4.7 %template.1 = (f32[8,32,2048]{2,1,0:T(8,128)}, f32[32,2048]{1,0:T(8,128)}, f32[21,32]{1,0:T(8,128)}, s32[32,128]{1,0:T(8,128)}, bf16[32,4096]{1,0:T(8,128)(2,1)}, /*index=5*/f32[6,8,2048]{2,1,0:T(8,128)}) custom-call(s32[32,128]{1,0:T(8,128)} %bitcast.14, bf16[32,8,2048]{2,1,0:T(8,128)(2,1)} %stiff_ref.1, f32[3,8,2048]{2,1,0:T(8,128)} %nrm_ref.3, ...), custom_call_target="tpu_custom_call" | custom-call | flops 40000000 | bytes 8000000 | tf_op jit(solution)/shard_map/template/pallas_call | solution.py:546
  11.4 0.0 collective-permute-done
  11.4 0.0 copy-start
  11.4 0.6 %copy-done = f32[3,1,4,128]{3,2,0,1:T(4,128)} copy-done((f32[3,1,4,128]{3,2,0,1:T(4,128)}, f32[3,1,4,128]{3,2,0,1:T(4,128)S(1)}, u32[]{:S(2)}) %copy-start) | copy-done | bytes 6168
  12.0 18.0 %relax.1 = (f32[3,4,128]{2,1,0:T(4,128)}, f32[3,4,128]{2,1,0:T(4,128)}, f32[192,128]{1,0:T(8,128)}, f32[6,32]{1,0:T(8,128)}) custom-call(f32[3,4,128]{2,1,0:T(4,128)} %bitcast.16, f32[3,4,128]{2,1,0:T(4,128)} %bitcast.18, f32[3,4,128]{2,1,0:T(4,128)} %bitcast.17, bf16[672,128]{1,0:T(8,128)(2,1)} %bitcast.13, s32[32,128]{1,0:T(8,128)} %get-tuple-element.14.rank_ref, ...), custom_call_target="tpu_custom_call" | custom-call | flops 200000000 | bytes 8000000 | tf_op jit(solution)/shard_map/relax/pallas_call | solution.py:571
  30.0 1.9 %collective-permute-start.1 = (f32[3,4,128]{2,1,0:T(4,128)}, f32[3,4,128]{2,1,0:T(4,128)S(1)}, u32[]{:S(2)}, u32[]{:S(2)}) collective-permute-start(f32[3,4,128]{2,1,0:T(4,128)} %get-tuple-element.21), channel_id=1, source_target_pairs={{0,1},{1,2},{2,3},{3,4},{4,5},{5,6},{6,7},{7,8},{8,9},{9,10},{10,1... | collective-permute-start | bytes 18440 | tf_op jit(solution)/shard_map/ppermute | solution.py:26
  32.0 8.7 %collective-permute-done.1 = f32[3,4,128]{2,1,0:T(4,128)S(1)} collective-permute-done((f32[3,4,128]{2,1,0:T(4,128)}, f32[3,4,128]{2,1,0:T(4,128)S(1)}, u32[]{:S(2)}, u32[]{:S(2)}) %collective-permute-start.1) | collective-permute-done | bytes 6176 | tf_op jit(solution)/shard_map/ppermute | solution.py:26
  40.6 1.3 %subtract_bitcast_fusion = f32[3,1,4,128]{3,2,1,0:T(4,128)} fusion(f32[3,4,128]{2,1,0:T(4,128)} %get-tuple-element.20, f32[3,4,128]{2,1,0:T(4,128)S(1)} %collective-permute-done.1), kind=kLoop, calls=%fused_computation | loop fusion | flops 1536 | bytes 18432
Async XLA Ops:
  0.6 10.8 %collective-permute-start = (f32[3,1,4,128]{3,2,0,1:T(4,128)}, f32[3,1,4,128]{3,2,0,1:T(4,128)S(1)}, u32[]{:S(2)}, u32[]{:S(2)}) collective-permute-start(f32[3,1,4,128]{3,2,0,1:T(4,128)} %bitcast.15), channel_id=1, source_target_pairs={{1,0},{2,1},{3,2},{4,3},{5,4},{6,5},{7,6},{8,7},{9,8},{10,9},{11,1... | collective-permute-start | bytes 18440 | tf_op jit(solution)/shard_map/ppermute | solution.py:26
  11.4 0.6 %copy-start = (f32[3,1,4,128]{3,2,0,1:T(4,128)}, f32[3,1,4,128]{3,2,0,1:T(4,128)S(1)}, u32[]{:S(2)}) copy-start(f32[3,1,4,128]{3,2,0,1:T(4,128)S(1)} %collective-permute-done) | copy-start | bytes 18436
  30.0 10.6 %collective-permute-start.1 = (f32[3,4,128]{2,1,0:T(4,128)}, f32[3,4,128]{2,1,0:T(4,128)S(1)}, u32[]{:S(2)}, u32[]{:S(2)}) collective-permute-start(f32[3,4,128]{2,1,0:T(4,128)} %get-tuple-element.21), channel_id=1, source_target_pairs={{0,1},{1,2},{2,3},{3,4},{4,5},{5,6},{6,7},{7,8},{8,9},{9,10},{10,1... | collective-permute-start | bytes 18440 | tf_op jit(solution)/shard_map/ppermute | solution.py:26

commit v3 on v2

--- a/solution.py
+++ b/solution.py
@@ -54,22 +54,64 @@
 
 
 def template_kernel(
-    flags_ref,
-    stiff_ref,
-    nrm_ref,
-    br_ref,
-    nbr_ref,
+    flags_hbm,
+    stiff_hbm,
+    nrm_hbm,
+    br_hbm,
+    nbr_hbm,
+    disp_hbm,
+    load_hbm,
+    tangent_hbm,
     wt_ref,
     cd_ref,
     tan_ref,
+    tan_copy_ref,
     rank_ref,
     sel_ref,
     lp_ref,
+    nrm_ref,
+    nbr_ref,
+    disp_ref,
+    load_ref,
+    tangent_ref,
     raw_ref,
     basis_ref,
     high_ref,
     low_ref,
+    flags_ref,
+    stiff_ref,
+    br_ref,
+    small_sems,
+    stiff_sems,
 ):
+    small = [
+        pltpu.make_async_copy(source, target, small_sems.at[place])
+        for place, (source, target) in enumerate(
+            [
+                (flags_hbm, flags_ref),
+                (nrm_hbm, nrm_ref),
+                (br_hbm, br_ref),
+                (nbr_hbm, nbr_ref),
+                (disp_hbm, disp_ref),
+                (load_hbm, load_ref),
+                (tangent_hbm, tangent_ref),
+            ]
+        )
+    ]
+    quarter = GRAINS // 4
+    big = [
+        pltpu.make_async_copy(
+            stiff_hbm.at[:, :, pl.ds(part * quarter, quarter)],
+            stiff_ref.at[:, :, pl.ds(part * quarter, quarter)],
+            stiff_sems.at[part],
+        )
+        for part in range(4)
+    ]
+    for copy in small[:4] + big + small[4:]:
+        copy.start()
+    for copy in small[:4]:
+        copy.wait()
+
     flags = flags_ref[...]
     flags_f = flags.astype(jnp.float32)
     tri = (
@@ -124,7 +166,9 @@
             cd_ref[group * 8 : (group + 1) * 8, lanes] = RELAX_FACTOR / total
         return carry
 
-    lax.fori_loop(0, CHUNKS, chunk_step, 0)
+    for part in range(4):
+        big[part].wait()
+        lax.fori_loop(part * CHUNKS // 4, (part + 1) * CHUNKS // 4, chunk_step, 0)
 
     acc = jnp.zeros((32, 32), jnp.float32)
     for contact in range(CONTACTS):
@@ -136,6 +180,9 @@
     slot_lane = lax.broadcasted_iota(jnp.int32, (32, 32), 1).astype(jnp.float32)
     acc = jnp.where(slot_lane < live_total, acc * (1.0 / GRAINS), 0.0)
     tan_ref[...] = acc[:21]
+    tan_copy_ref[...] = acc[:21]
+    for copy in small[4:]:
+        copy.wait()
 
 
 def lerp(low_value, high_value, bit):
@@ -539,31 +586,48 @@
 
 
 VMEM = pl.BlockSpec(memory_space=pltpu.VMEM)
-
-
-def run_template(flags, stiffness, normals, branch_length, neighbours):
+HBM = pl.BlockSpec(memory_space=pltpu.HBM)
+
+
+def run_template(
+    flags, stiffness, normals, branch_length, neighbours, displacement, load, elastic_tangent
+):
     f32 = jnp.float32
+    kept = [normals, neighbours, displacement, load, elastic_tangent]
     return pl.pallas_call(
         template_kernel,
         out_shape=(
             jax.ShapeDtypeStruct((CONTACTS, SLOT_COUNT, GRAINS), f32),
             jax.ShapeDtypeStruct((SLOT_COUNT, GRAINS), f32),
             jax.ShapeDtypeStruct((21, SLOT_COUNT), f32),
+            jax.ShapeDtypeStruct((21, SLOT_COUNT), f32),
             jax.ShapeDtypeStruct((32, 128), jnp.int32),
             jax.ShapeDtypeStruct((SLOT_COUNT, 4096), jnp.bfloat16),
             jax.ShapeDtypeStruct((6, CONTACTS, GRAINS), f32),
-        ),
-        in_specs=[VMEM] * 5,
-        out_specs=(VMEM,) * 6,
+        )
+        + tuple(jax.ShapeDtypeStruct(value.shape, value.dtype) for value in kept),
+        in_specs=[HBM] * 8,
+        out_specs=(VMEM,) * 12,
         scratch_shapes=[
             pltpu.VMEM((SLOT_COUNT * CONTACTS, 128), f32),
             pltpu.VMEM((256, 128), f32),
             pltpu.VMEM((CONTACTS, 32, GRAINS), jnp.bfloat16),
             pltpu.VMEM((CONTACTS, 32, GRAINS), jnp.bfloat16),
+            pltpu.VMEM((32, 128), jnp.int32),
+            pltpu.VMEM((SLOT_COUNT, CONTACTS, GRAINS), jnp.bfloat16),
+            pltpu.VMEM((CONTACTS, GRAINS), f32),
+            pltpu.SemaphoreType.DMA((7,)),
+            pltpu.SemaphoreType.DMA((4,)),
         ],
         cost_estimate=pl.CostEstimate(flops=40_000_000, bytes_accessed=8_000_000, transcendentals=0),
+        compiler_params=pltpu.CompilerParams(vmem_limit_bytes=16 * 1024 * 1024),
         name="template",
-    )(flags, stiffness, normals, branch_length, neighbours)
+    )(
+        *[
+            pltpu.with_memory_space_constraint(value, pltpu.HBM)
+            for value in (flags, stiffness, *kept[:1], branch_length, *kept[1:])
+        ]
+    )
 
 
 def run_relax(disp, upper, load, tangent, rank, sel, wt, cd, lp, normals, neighbours, tan):
@@ -595,6 +659,7 @@
         cost_estimate=pl.CostEstimate(
             flops=200_000_000, bytes_accessed=8_000_000, transcendentals=0
         ),
+        compiler_params=pltpu.CompilerParams(vmem_limit_bytes=28 * 1024 * 1024),
         name="relax",
     )(disp, upper, load, tangent, rank, sel, wt, cd, lp, normals, neighbours, tan)
 
@@ -610,22 +675,18 @@
     neighbours,
 ):
     upper = shifted(displacement, ("row", "col"), -1)
-    wt, cd, tangent, rank, sel, lp = run_template(
-        band_flags.reshape(32, 128), contact_stiffness, normals, branch_length, neighbours
+    wt, cd, tangent, tan, rank, sel, lp, nrm, nbr, disp, load_here, elastic = run_template(
+        band_flags.reshape(32, 128),
+        contact_stiffness,
+        normals,
+        branch_length,
+        neighbours,
+        displacement.reshape(3, 4, 128),
+        load.reshape(3, 4, 128),
+        elastic_tangent.reshape(672, 128),
     )
     pre, carried, stress, band = run_relax(
-        displacement.reshape(3, 4, 128),
-        upper.reshape(3, 4, 128),
-        load.reshape(3, 4, 128),
-        elastic_tangent.reshape(672, 128),
-        rank,
-        sel,
-        wt,
-        cd,
-        lp,
-        normals,
-        neighbours,
-        tangent,
+        disp, upper.reshape(3, 4, 128), load_here, elastic, rank, sel, wt, cd, lp, nrm, nbr, tan
     )
     arrived = shifted(carried, ("row", "col"), 1)
     residual = (pre - arrived).reshape(3, 1, 4, 128)

time: 42.1 us -> 38 us (0.903)
  Pallas kernels: 22.7 us -> 20 us
  other arithmetic: 1.29 us -> 0.6 us
  local copies, waits for them, and re-layouts: 0.59 us -> 0 us
    pallas_call x1, Pallas kernels: 18 us -> 15.8 us  [run_relax(): pl.pallas_call(relax_kernel, out_shape=(jax.ShapeDtypeStruct((3, 4, 128),...]
    unnamed x1, other arithmetic: 1.29 us -> 0.6 us
    unnamed x2 -> x0, local copies, waits for them, and re-layouts: 0.59 us -> none
    pallas_call x1, Pallas kernels: 4.66 us -> 4.22 us  [run_template(): pl.pallas_call(template_kernel, out_shape=(jax.ShapeDtypeStruct((CONTACTS...]
where the time goes in v3:
time: 38 us; the launch traced here: 37.8 us
  Pallas kernels  20 us (53%)
  waiting for transfers between devices  8.45 us (22%)
  starting transfers between devices  8.01 us (21%)
  between operations  0.67 us (2%)
  other arithmetic  0.6 us (2%)
    pallas_call x1, Pallas kernels, run_relax(): pl.pallas_call(relax_kernel, out_shape=(jax.ShapeDtypeStruct((3, 4, 128),...  15.8 us
    ppermute x2, waiting for transfers between devices, shifted(): lax.ppermute(value, axis, [(source, source + steps) for source in range(l...  8.45 us
    ppermute x2, starting transfers between devices, shifted(): lax.ppermute(value, axis, [(source, source + steps) for source in range(l...  8.01 us
    pallas_call x1, Pallas kernels, run_template(): pl.pallas_call(template_kernel, out_shape=(jax.ShapeDtypeStruct((CONTACTS...  4.22 us
  transfers between devices with their start and end apart: 2, of which 1 were waited for; matrix products, arithmetic and copies ran while one was open for 0% of the time, Pallas kernels for 11%

profile of v3, /device:TPU:128, one launch (start us, length us, event | category | flops | bytes accessed | tf_op | source)
XLA Modules:
  0.0 37.8 jit_solution(6225671319147515470)
XLA Ops:
  0.6 6.1 %collective-permute-start = (f32[3,1,4,128]{3,2,0,1:T(4,128)}, f32[3,1,4,128]{3,2,0,1:T(4,128)S(1)}, u32[]{:S(2)}, u32[]{:S(2)}) collective-permute-start(f32[3,1,4,128]{3,2,0,1:T(4,128)} %bitcast.17), channel_id=1, source_target_pairs={{1,0},{2,1},{3,2},{4,3},{5,4},{6,5},{7,6},{8,7},{9,8},{10,9},{11,1... | collective-permute-start | bytes 18440 | tf_op jit(solution)/shard_map/ppermute | solution.py:26
  6.7 4.2 %template.1 = (f32[8,32,2048]{2,1,0:T(8,128)S(1)}, f32[32,2048]{1,0:T(8,128)S(1)}, f32[21,32]{1,0:T(8,128)}, f32[21,32]{1,0:T(8,128)S(1)}, s32[32,128]{1,0:T(8,1...) custom-call(s32[32,128]{1,0:T(8,128)} %bitcast.15, ...), custom_call_target="tpu_custom_call" | custom-call | flops 40000000 | bytes 8000000 | tf_op jit(solution)/shard_map/template/pallas_call | solution.py:597
  11.0 0.0 collective-permute-done
  11.0 15.8 %relax.1 = (f32[3,4,128]{2,1,0:T(4,128)S(1)}, f32[3,4,128]{2,1,0:T(4,128)S(1)}, f32[192,128]{1,0:T(8,128)}, f32[6,32]{1,0:T(8,128)}) custom-call(f32[3,4,128]{2,1,0:T(4,128)S(1)} %get-tuple-element.20.disp_ref, f32[3,4,128]{2,1,0:T(4,128)S(1)} %bitcast.13, f32[3,4,128]{2,1,0:T(4,128)S(1)} %get-tuple-element.21.load_ref, ...), custom_call_target="tpu_custom_call" | custom-call | flops 200000000 | bytes 8000000 | tf_op jit(solution)/shard_map/relax/pallas_call | solution.py:635
  26.8 1.9 %collective-permute-start.1 = (f32[3,4,128]{2,1,0:T(4,128)S(1)}, f32[3,4,128]{2,1,0:T(4,128)S(1)}, u32[]{:S(2)}, u32[]{:S(2)}) collective-permute-start(f32[3,4,128]{2,1,0:T(4,128)S(1)} %get-tuple-element.32), channel_id=1, source_target_pairs={{0,1},{1,2},{2,3},{3,4},{4,5},{5,6},{6,7},{7,8},{8,9},{9,10},{10,1... | collective-permute-start | bytes 18440 | tf_op jit(solution)/shard_map/ppermute | solution.py:26
  28.7 8.4 %collective-permute-done.1 = f32[3,4,128]{2,1,0:T(4,128)S(1)} collective-permute-done((f32[3,4,128]{2,1,0:T(4,128)S(1)}, f32[3,4,128]{2,1,0:T(4,128)S(1)}, u32[]{:S(2)}, u32[]{:S(2)}) %collective-permute-start.1) | collective-permute-done | bytes 6176 | tf_op jit(solution)/shard_map/ppermute | solution.py:26
  37.2 0.6 %subtract_bitcast_fusion = f32[3,1,4,128]{3,2,1,0:T(4,128)} fusion(f32[3,4,128]{2,1,0:T(4,128)S(1)} %get-tuple-element.31, f32[3,4,128]{2,1,0:T(4,128)S(1)} %collective-permute-done.1), kind=kLoop, calls=%fused_computation | loop fusion | flops 1536 | bytes 18432
Async XLA Ops:
  0.6 10.3 %collective-permute-start = (f32[3,1,4,128]{3,2,0,1:T(4,128)}, f32[3,1,4,128]{3,2,0,1:T(4,128)S(1)}, u32[]{:S(2)}, u32[]{:S(2)}) collective-permute-start(f32[3,1,4,128]{3,2,0,1:T(4,128)} %bitcast.17), channel_id=1, source_target_pairs={{1,0},{2,1},{3,2},{4,3},{5,4},{6,5},{7,6},{8,7},{9,8},{10,9},{11,1... | collective-permute-start | bytes 18440 | tf_op jit(solution)/shard_map/ppermute | solution.py:26
  26.8 10.4 %collective-permute-start.1 = (f32[3,4,128]{2,1,0:T(4,128)S(1)}, f32[3,4,128]{2,1,0:T(4,128)S(1)}, u32[]{:S(2)}, u32[]{:S(2)}) collective-permute-start(f32[3,4,128]{2,1,0:T(4,128)S(1)} %get-tuple-element.32), channel_id=1, source_target_pairs={{0,1},{1,2},{2,3},{3,4},{4,5},{5,6},{6,7},{7,8},{8,9},{9,10},{10,1... | collective-permute-start | bytes 18440 | tf_op jit(solution)/shard_map/ppermute | solution.py:26

commit v4 on v3

--- a/solution.py
+++ b/solution.py
@@ -16,6 +16,7 @@
 GROUPS = SLOT_COUNT // 8
 CHUNKS = GRAINS // 128
 UNROLL = 4
+EXACT = False
 PAIRS = [(row_id, col_id) for row_id in range(6) for col_id in range(row_id, 6)]
 NT = (((1,), (1,)), ((), ()))
 
@@ -76,8 +77,7 @@
     tangent_ref,
     raw_ref,
     basis_ref,
-    high_ref,
-    low_ref,
+    split_ref,
     flags_ref,
     stiff_ref,
     br_ref,
@@ -151,8 +151,10 @@
         for contact in range(CONTACTS):
             basis = basis_ref[pl.ds(contact, 32, stride=8), :]
             high = basis.astype(jnp.bfloat16)
-            high_ref[contact, :, lanes] = high
-            low_ref[contact, :, lanes] = (basis - high.astype(jnp.float32)).astype(jnp.bfloat16)
+            split_ref[contact, 0:32, lanes] = high
+            split_ref[contact, 32:64, lanes] = (basis - high.astype(jnp.float32)).astype(
+                jnp.bfloat16
+            )
         for slot in range(SLOT_COUNT):
             raw_ref[slot * 8 : (slot + 1) * 8, :] = (
                 stiff_ref[slot, :, lanes].astype(jnp.float32) * mask
@@ -170,13 +172,13 @@
         big[part].wait()
         lax.fori_loop(part * CHUNKS // 4, (part + 1) * CHUNKS // 4, chunk_step, 0)
 
-    acc = jnp.zeros((32, 32), jnp.float32)
+    acc = jnp.zeros((64, 32), jnp.float32)
     for contact in range(CONTACTS):
         weights = wt_ref[contact].astype(jnp.bfloat16)
-        for part_ref in (high_ref, low_ref):
-            acc = acc + lax.dot_general(
-                part_ref[contact], weights, NT, preferred_element_type=jnp.float32
-            )
+        acc = acc + lax.dot_general(
+            split_ref[contact], weights, NT, preferred_element_type=jnp.float32
+        )
+    acc = acc[0:32] + acc[32:64]
     slot_lane = lax.broadcasted_iota(jnp.int32, (32, 32), 1).astype(jnp.float32)
     acc = jnp.where(slot_lane < live_total, acc * (1.0 / GRAINS), 0.0)
     tan_ref[...] = acc[:21]
@@ -400,7 +402,7 @@
 
     tall = lax.broadcasted_iota(jnp.int32, (96, 128), 1) < 64
 
-    def dot_pieces(source_ref, chunk):
+    def dot_pieces(source_ref, chunk, exact):
         lanes = lanes_of(chunk)
         lanes_up = lanes_of((chunk + 1) & (CHUNKS - 1))
         lanes_down = lanes_of((chunk + CHUNKS - 1) & (CHUNKS - 1))
@@ -408,12 +410,15 @@
         sides = jnp.where(tall, source_ref[:, lanes_up], source_ref[:, lanes_down])
         window = jnp.concatenate([own, sides], axis=1)
         high = window.astype(jnp.bfloat16)
-        low = (window - high.astype(jnp.float32)).astype(jnp.bfloat16)
-        both = jnp.concatenate([high, low], axis=0)
+        if exact:
+            low = (window - high.astype(jnp.float32)).astype(jnp.bfloat16)
+            both = jnp.concatenate([high, low], axis=0)
 
         def pieces(pair):
             place = chunk * CONTACTS + 2 * pair
             picks = jnp.concatenate([onehot_ref[place], onehot_ref[place + 1]], axis=1)
+            if not exact:
+                return jnp.dot(high, picks, preferred_element_type=jnp.float32)
             value = jnp.dot(both, picks, preferred_element_type=jnp.float32)
             return value[0:96] + value[96:192]
 
@@ -471,16 +476,18 @@
 
         lax.fori_loop(0, CONTACTS, contact_step, 0)
 
-    def all_chunks(source_ref, work):
+    def all_chunks(source_ref, work, exact):
+        unroll = 4 if exact else 8
+
         @pl.when(all_near)
         def _():
             def step(turn, carry):
-                for place in range(UNROLL):
-                    chunk = turn * UNROLL + place
-                    work(chunk, dot_pieces(source_ref, chunk))
+                for place in range(unroll):
+                    chunk = turn * unroll + place
+                    work(chunk, dot_pieces(source_ref, chunk, exact))
                 return carry
 
-            lax.fori_loop(0, CHUNKS // UNROLL, step, 0)
+            lax.fori_loop(0, CHUNKS // unroll, step, 0)
 
         @pl.when(jnp.logical_not(all_near))
         def _():
@@ -519,7 +526,7 @@
                     rows = slice(tile * 8, (tile + 1) * 8)
                     target_ref[rows, lanes] = own[tile] + first_ref[rows, lanes] + factor * totals[tile]
 
-        all_chunks(source_ref, work)
+        all_chunks(source_ref, work, EXACT)
 
     def stress_work(chunk, pieces):
         lanes = lanes_of(chunk)
@@ -540,7 +547,7 @@
         target = fluct_b_ref if turn % 2 else fluct_a_ref
         sweep(current, target)
         current = target
-    all_chunks(current, stress_work)
+    all_chunks(current, stress_work, True)
 
     lane32 = lax.broadcasted_iota(jnp.int32, (32, 128), 1)
     table = jnp.zeros((32, 128), jnp.float32)
@@ -611,8 +618,7 @@
         scratch_shapes=[
             pltpu.VMEM((SLOT_COUNT * CONTACTS, 128), f32),
             pltpu.VMEM((256, 128), f32),
-            pltpu.VMEM((CONTACTS, 32, GRAINS), jnp.bfloat16),
-            pltpu.VMEM((CONTACTS, 32, GRAINS), jnp.bfloat16),
+            pltpu.VMEM((CONTACTS, 64, GRAINS), jnp.bfloat16),
             pltpu.VMEM((32, 128), jnp.int32),
             pltpu.VMEM((SLOT_COUNT, CONTACTS, GRAINS), jnp.bfloat16),
             pltpu.VMEM((CONTACTS, GRAINS), f32),

time: 38 us -> 36.6 us (0.963)
  Pallas kernels: 20 us -> 18.7 us
    pallas_call x1, Pallas kernels: 15.8 us -> 14.5 us  [run_relax(): pl.pallas_call(relax_kernel, out_shape=(jax.ShapeDtypeStruct((3, 4, 128),...]
  transfers between devices with their start and end apart: 2 -> 2, of which waited for: 1 -> 1; matrix products, arithmetic and copies ran while one was open for 0% -> 0% of each run, Pallas kernels for 11% -> 12%
where the time goes in v4:
time: 36.6 us; the launch traced here: 36.4 us
  Pallas kernels  18.7 us (51%)
  waiting for transfers between devices  8.45 us (23%)
  starting transfers between devices  8.01 us (22%)
  between operations  0.67 us (2%)
  other arithmetic  0.6 us (2%)
    pallas_call x1, Pallas kernels, run_relax(): pl.pallas_call(relax_kernel, out_shape=(jax.ShapeDtypeStruct((3, 4, 128),...  14.5 us
    ppermute x2, waiting for transfers between devices, shifted(): lax.ppermute(value, axis, [(source, source + steps) for source in range(l...  8.45 us
    ppermute x2, starting transfers between devices, shifted(): lax.ppermute(value, axis, [(source, source + steps) for source in range(l...  8.01 us
    pallas_call x1, Pallas kernels, run_template(): pl.pallas_call(template_kernel, out_shape=(jax.ShapeDtypeStruct((CONTACTS...  4.19 us
  transfers between devices with their start and end apart: 2, of which 1 were waited for; matrix products, arithmetic and copies ran while one was open for 0% of the time, Pallas kernels for 12%

profile of v4, /device:TPU:128, one launch (start us, length us, event | category | flops | bytes accessed | tf_op | source)
XLA Modules:
  0.0 36.4 jit_solution(12635228242137988162)
XLA Ops:
  0.6 6.1 %collective-permute-start = (f32[3,1,4,128]{3,2,0,1:T(4,128)}, f32[3,1,4,128]{3,2,0,1:T(4,128)S(1)}, u32[]{:S(2)}, u32[]{:S(2)}) collective-permute-start(f32[3,1,4,128]{3,2,0,1:T(4,128)} %bitcast.17), channel_id=1, source_target_pairs={{1,0},{2,1},{3,2},{4,3},{5,4},{6,5},{7,6},{8,7},{9,8},{10,9},{11,1... | collective-permute-start | bytes 18440 | tf_op jit(solution)/shard_map/ppermute | solution.py:27
  6.7 4.2 %template.1 = (f32[8,32,2048]{2,1,0:T(8,128)S(1)}, f32[32,2048]{1,0:T(8,128)S(1)}, f32[21,32]{1,0:T(8,128)}, f32[21,32]{1,0:T(8,128)S(1)}, s32[32,128]{1,0:T(8,1...) custom-call(s32[32,128]{1,0:T(8,128)} %bitcast.15, ...), custom_call_target="tpu_custom_call" | custom-call | flops 40000000 | bytes 8000000 | tf_op jit(solution)/shard_map/template/pallas_call | solution.py:604
  10.9 0.0 collective-permute-done
  11.0 14.5 %relax.1 = (f32[3,4,128]{2,1,0:T(4,128)S(1)}, f32[3,4,128]{2,1,0:T(4,128)S(1)}, f32[192,128]{1,0:T(8,128)}, f32[6,32]{1,0:T(8,128)}) custom-call(f32[3,4,128]{2,1,0:T(4,128)S(1)} %get-tuple-element.20.disp_ref, f32[3,4,128]{2,1,0:T(4,128)S(1)} %bitcast.13, f32[3,4,128]{2,1,0:T(4,128)S(1)} %get-tuple-element.21.load_ref, ...), custom_call_target="tpu_custom_call" | custom-call | flops 200000000 | bytes 8000000 | tf_op jit(solution)/shard_map/relax/pallas_call | solution.py:641
  25.4 1.9 %collective-permute-start.1 = (f32[3,4,128]{2,1,0:T(4,128)S(1)}, f32[3,4,128]{2,1,0:T(4,128)S(1)}, u32[]{:S(2)}, u32[]{:S(2)}) collective-permute-start(f32[3,4,128]{2,1,0:T(4,128)S(1)} %get-tuple-element.32), channel_id=1, source_target_pairs={{0,1},{1,2},{2,3},{3,4},{4,5},{5,6},{6,7},{7,8},{8,9},{9,10},{10,1... | collective-permute-start | bytes 18440 | tf_op jit(solution)/shard_map/ppermute | solution.py:27
  27.3 8.4 %collective-permute-done.1 = f32[3,4,128]{2,1,0:T(4,128)S(1)} collective-permute-done((f32[3,4,128]{2,1,0:T(4,128)S(1)}, f32[3,4,128]{2,1,0:T(4,128)S(1)}, u32[]{:S(2)}, u32[]{:S(2)}) %collective-permute-start.1) | collective-permute-done | bytes 6176 | tf_op jit(solution)/shard_map/ppermute | solution.py:27
  35.8 0.6 %subtract_bitcast_fusion = f32[3,1,4,128]{3,2,1,0:T(4,128)} fusion(f32[3,4,128]{2,1,0:T(4,128)S(1)} %get-tuple-element.31, f32[3,4,128]{2,1,0:T(4,128)S(1)} %collective-permute-done.1), kind=kLoop, calls=%fused_computation | loop fusion | flops 1536 | bytes 18432
Async XLA Ops:
  0.6 10.3 %collective-permute-start = (f32[3,1,4,128]{3,2,0,1:T(4,128)}, f32[3,1,4,128]{3,2,0,1:T(4,128)S(1)}, u32[]{:S(2)}, u32[]{:S(2)}) collective-permute-start(f32[3,1,4,128]{3,2,0,1:T(4,128)} %bitcast.17), channel_id=1, source_target_pairs={{1,0},{2,1},{3,2},{4,3},{5,4},{6,5},{7,6},{8,7},{9,8},{10,9},{11,1... | collective-permute-start | bytes 18440 | tf_op jit(solution)/shard_map/ppermute | solution.py:27
  25.4 10.4 %collective-permute-start.1 = (f32[3,4,128]{2,1,0:T(4,128)S(1)}, f32[3,4,128]{2,1,0:T(4,128)S(1)}, u32[]{:S(2)}, u32[]{:S(2)}) collective-permute-start(f32[3,4,128]{2,1,0:T(4,128)S(1)} %get-tuple-element.32), channel_id=1, source_target_pairs={{0,1},{1,2},{2,3},{3,4},{4,5},{5,6},{6,7},{7,8},{8,9},{9,10},{10,1... | collective-permute-start | bytes 18440 | tf_op jit(solution)/shard_map/ppermute | solution.py:27

commit v5 on v4

--- a/solution.py
+++ b/solution.py
@@ -66,7 +66,6 @@
     wt_ref,
     cd_ref,
     tan_ref,
-    tan_copy_ref,
     rank_ref,
     sel_ref,
     lp_ref,
@@ -182,7 +181,6 @@
     slot_lane = lax.broadcasted_iota(jnp.int32, (32, 32), 1).astype(jnp.float32)
     acc = jnp.where(slot_lane < live_total, acc * (1.0 / GRAINS), 0.0)
     tan_ref[...] = acc[:21]
-    tan_copy_ref[...] = acc[:21]
     for copy in small[4:]:
         copy.wait()
 
@@ -275,7 +273,6 @@
 def relax_kernel(
     disp_ref,
     upper_ref,
-    load_ref,
     tangent_ref,
     rank_ref,
     sel_ref,
@@ -285,7 +282,6 @@
     nrm_ref,
     nbr_ref,
     tan_ref,
-    pre_ref,
     carried_ref,
     stress_ref,
     band_ref,
@@ -584,12 +580,24 @@
         value = jnp.where(banded, values, running)
         stress_ref[row_id * 32 : (row_id + 1) * 32, :] = value
         stress.append(value)
-    planes = force_rows(
-        [[stress[comp][point * 8 : (point + 1) * 8, :] for comp in range(6)] for point in range(4)]
-    )
+    planes = force_rows(tiles_of(stress))
+    for axis_id in range(3):
+        carried_ref[axis_id] = planes[1][axis_id][0:4]
+
+
+def tiles_of(stress):
+    return [
+        [stress[comp][point * 8 : (point + 1) * 8, :] for comp in range(6)] for point in range(4)
+    ]
+
+
+def output_kernel(stress_in, band_in, tan_in, load_ref, pre_ref, stress_ref, band_ref, tan_ref):
+    stress_ref[...] = stress_in[...]
+    band_ref[...] = band_in[...]
+    tan_ref[...] = tan_in[...]
+    planes = force_rows(tiles_of([stress_in[comp * 32 : (comp + 1) * 32, :] for comp in range(6)]))
     for axis_id in range(3):
         pre_ref[axis_id] = load_ref[axis_id] - planes[0][axis_id][0:4]
-        carried_ref[axis_id] = planes[1][axis_id][0:4]
 
 
 VMEM = pl.BlockSpec(memory_space=pltpu.VMEM)
@@ -607,14 +615,13 @@
             jax.ShapeDtypeStruct((CONTACTS, SLOT_COUNT, GRAINS), f32),
             jax.ShapeDtypeStruct((SLOT_COUNT, GRAINS), f32),
             jax.ShapeDtypeStruct((21, SLOT_COUNT), f32),
-            jax.ShapeDtypeStruct((21, SLOT_COUNT), f32),
             jax.ShapeDtypeStruct((32, 128), jnp.int32),
             jax.ShapeDtypeStruct((SLOT_COUNT, 4096), jnp.bfloat16),
             jax.ShapeDtypeStruct((6, CONTACTS, GRAINS), f32),
         )
         + tuple(jax.ShapeDtypeStruct(value.shape, value.dtype) for value in kept),
         in_specs=[HBM] * 8,
-        out_specs=(VMEM,) * 12,
+        out_specs=(VMEM,) * 11,
         scratch_shapes=[
             pltpu.VMEM((SLOT_COUNT * CONTACTS, 128), f32),
             pltpu.VMEM((256, 128), f32),
@@ -636,18 +643,17 @@
     )
 
 
-def run_relax(disp, upper, load, tangent, rank, sel, wt, cd, lp, normals, neighbours, tan):
+def run_relax(disp, upper, tangent, rank, sel, wt, cd, lp, normals, neighbours, tan):
     f32 = jnp.float32
     return pl.pallas_call(
         relax_kernel,
         out_shape=(
             jax.ShapeDtypeStruct((3, 4, 128), f32),
-            jax.ShapeDtypeStruct((3, 4, 128), f32),
             jax.ShapeDtypeStruct((192, 128), f32),
             jax.ShapeDtypeStruct((6, SLOT_COUNT), f32),
         ),
-        in_specs=[VMEM] * 12,
-        out_specs=(VMEM,) * 4,
+        in_specs=[VMEM] * 11,
+        out_specs=(VMEM,) * 3,
         scratch_shapes=[
             pltpu.VMEM((8, 128), f32),
             pltpu.VMEM((256, 128), f32),
@@ -667,7 +673,25 @@
         ),
         compiler_params=pltpu.CompilerParams(vmem_limit_bytes=28 * 1024 * 1024),
         name="relax",
-    )(disp, upper, load, tangent, rank, sel, wt, cd, lp, normals, neighbours, tan)
+    )(disp, upper, tangent, rank, sel, wt, cd, lp, normals, neighbours, tan)
+
+
+def run_output(stress, band, tan, load):
+    f32 = jnp.float32
+    return pl.pallas_call(
+        output_kernel,
+        out_shape=(
+            jax.ShapeDtypeStruct((3, 4, 128), f32),
+            jax.ShapeDtypeStruct((192, 128), f32),
+            jax.ShapeDtypeStruct((6, SLOT_COUNT), f32),
+            jax.ShapeDtypeStruct((21, SLOT_COUNT), f32),
+        ),
+        in_specs=[VMEM] * 4,
+        out_specs=(VMEM,) * 4,
+        cost_estimate=pl.CostEstimate(flops=1_000_000, bytes_accessed=2_000_000, transcendentals=0),
+        compiler_params=pltpu.CompilerParams(vmem_limit_bytes=8 * 1024 * 1024),
+        name="output",
+    )(stress, band, tan, load)
 
 
 def body(
@@ -681,7 +705,7 @@
     neighbours,
 ):
     upper = shifted(displacement, ("row", "col"), -1)
-    wt, cd, tangent, tan, rank, sel, lp, nrm, nbr, disp, load_here, elastic = run_template(
+    wt, cd, tan, rank, sel, lp, nrm, nbr, disp, load_here, elastic = run_template(
         band_flags.reshape(32, 128),
         contact_stiffness,
         normals,
@@ -691,10 +715,11 @@
         load.reshape(3, 4, 128),
         elastic_tangent.reshape(672, 128),
     )
-    pre, carried, stress, band = run_relax(
-        disp, upper.reshape(3, 4, 128), load_here, elastic, rank, sel, wt, cd, lp, nrm, nbr, tan
+    carried, stress_here, band_here = run_relax(
+        disp, upper.reshape(3, 4, 128), elastic, rank, sel, wt, cd, lp, nrm, nbr, tan
     )
     arrived = shifted(carried, ("row", "col"), 1)
+    pre, stress, band, tangent = run_output(stress_here, band_here, tan, load_here)
     residual = (pre - arrived).reshape(3, 1, 4, 128)
     return (residual, stress.reshape(6, 8, 1, 4, 128), tangent, band)
 

time: 36.6 us -> 35.5 us (0.970)
  waiting for transfers between devices: 8.45 us -> 7.79 us
  Pallas kernels: 18.7 us -> 18.2 us
    ppermute x2, waiting for transfers between devices: 8.45 us -> 7.79 us  [shifted(): lax.ppermute(value, axis, [(source, source + steps) for source in range(l...]
    pallas_call x0 -> x1, Pallas kernels: none -> 0.66 us  [run_output(): pl.pallas_call(output_kernel, out_shape=(jax.ShapeDtypeStruct((3, 4, 128)...]
    pallas_call x1, Pallas kernels: 4.19 us -> 3.59 us  [run_template(): pl.pallas_call(template_kernel, out_shape=(jax.ShapeDtypeStruct((CONTACTS...]
    pallas_call x1, Pallas kernels: 14.5 us -> 13.9 us  [run_relax(): pl.pallas_call(relax_kernel, out_shape=(jax.ShapeDtypeStruct((3, 4, 128),...]
where the time goes in v5:
time: 35.5 us; the launch traced here: 35.3 us
  Pallas kernels  18.2 us (51%)
  starting transfers between devices  8.02 us (23%)
  waiting for transfers between devices  7.79 us (22%)
  between operations  0.67 us (2%)
  other arithmetic  0.6 us (2%)
    pallas_call x1, Pallas kernels, run_relax(): pl.pallas_call(relax_kernel, out_shape=(jax.ShapeDtypeStruct((3, 4, 128),...  13.9 us
    ppermute x2, starting transfers between devices, shifted(): lax.ppermute(value, axis, [(source, source + steps) for source in range(l...  8.02 us
    ppermute x2, waiting for transfers between devices, shifted(): lax.ppermute(value, axis, [(source, source + steps) for source in range(l...  7.79 us
    pallas_call x1, Pallas kernels, run_template(): pl.pallas_call(template_kernel, out_shape=(jax.ShapeDtypeStruct((CONTACTS...  3.59 us
  transfers between devices with their start and end apart: 2, of which 1 were waited for; matrix products, arithmetic and copies ran while one was open for 0% of the time, Pallas kernels for 12%

profile of v5, /device:TPU:128, one launch (start us, length us, event | category | flops | bytes accessed | tf_op | source)
XLA Modules:
  0.0 35.3 jit_solution(4316683598354986289)
XLA Ops:
  0.6 6.1 %collective-permute-start = (f32[3,1,4,128]{3,2,0,1:T(4,128)}, f32[3,1,4,128]{3,2,0,1:T(4,128)S(1)}, u32[]{:S(2)}, u32[]{:S(2)}) collective-permute-start(f32[3,1,4,128]{3,2,0,1:T(4,128)} %bitcast.17), channel_id=1, source_target_pairs={{1,0},{2,1},{3,2},{4,3},{5,4},{6,5},{7,6},{8,7},{9,8},{10,9},{11,1... | collective-permute-start | bytes 18440 | tf_op jit(solution)/shard_map/ppermute | solution.py:27
  6.7 3.6 %template.1 = (f32[8,32,2048]{2,1,0:T(8,128)S(1)}, f32[32,2048]{1,0:T(8,128)S(1)}, f32[21,32]{1,0:T(8,128)S(1)}, s32[32,128]{1,0:T(8,128)S(1)}, bf16[32,4096]{1,...) custom-call(s32[32,128]{1,0:T(8,128)} %bitcast.15, ...), custom_call_target="tpu_custom_call" | custom-call | flops 40000000 | bytes 8000000 | tf_op jit(solution)/shard_map/template/pallas_call | solution.py:612
  10.3 0.0 collective-permute-done
  10.4 13.9 %relax.1 = (f32[3,4,128]{2,1,0:T(4,128)S(1)}, f32[192,128]{1,0:T(8,128)S(1)}, f32[6,32]{1,0:T(8,128)S(1)}) custom-call(f32[3,4,128]{2,1,0:T(4,128)S(1)} %get-tuple-element.22.disp_ref, f32[3,4,128]{2,1,0:T(4,128)S(1)} %bitcast.13, bf16[672,128]{1,0:T(8,128)(2,1)S(1)} %get-tuple-element.23.tangent_ref, s32[32,128]{1,0:T(8,128)S(1)} %get-tuple-element.24.rank_ref, ...), custom_call_target="tpu_custom_call" | custom-call | flops 200000000 | bytes 8000000 | tf_op jit(solution)/shard_map/relax/pallas_call | solution.py:648
  24.3 1.9 %collective-permute-start.1 = (f32[3,4,128]{2,1,0:T(4,128)S(1)}, f32[3,4,128]{2,1,0:T(4,128)S(1)}, u32[]{:S(2)}, u32[]{:S(2)}) collective-permute-start(f32[3,4,128]{2,1,0:T(4,128)S(1)} %get-tuple-element.36), channel_id=1, source_target_pairs={{0,1},{1,2},{2,3},{3,4},{4,5},{5,6},{6,7},{7,8},{8,9},{9,10},{10,1... | collective-permute-start | bytes 18440 | tf_op jit(solution)/shard_map/ppermute | solution.py:27
  26.2 0.7 %output.1 = (f32[3,4,128]{2,1,0:T(4,128)S(1)}, f32[192,128]{1,0:T(8,128)}, f32[6,32]{1,0:T(8,128)}, f32[21,32]{1,0:T(8,128)}) custom-call(f32[192,128]{1,0:T(8,128)S(1)} %get-tuple-element.32.stress_in, f32[6,32]{1,0:T(8,128)S(1)} %get-tuple-element.33.band_in, f32[21,32]{1,0:T(8,128)S(1)} %get-tuple-element.31.tan_ref.tan_in, ...), custom_call_target="tpu_custom_call" | custom-call | flops 1000000 | bytes 2000000 | tf_op jit(solution)/shard_map/output/pallas_call | solution.py:681
  26.9 7.8 %collective-permute-done.1 = f32[3,4,128]{2,1,0:T(4,128)S(1)} collective-permute-done((f32[3,4,128]{2,1,0:T(4,128)S(1)}, f32[3,4,128]{2,1,0:T(4,128)S(1)}, u32[]{:S(2)}, u32[]{:S(2)}) %collective-permute-start.1) | collective-permute-done | bytes 6176 | tf_op jit(solution)/shard_map/ppermute | solution.py:27
  34.7 0.6 %subtract_bitcast_fusion = f32[3,1,4,128]{3,2,1,0:T(4,128)} fusion(f32[3,4,128]{2,1,0:T(4,128)S(1)} %get-tuple-element.35, f32[3,4,128]{2,1,0:T(4,128)S(1)} %collective-permute-done.1), kind=kLoop, calls=%fused_computation | loop fusion | flops 1536 | bytes 18432
Async XLA Ops:
  0.6 9.7 %collective-permute-start = (f32[3,1,4,128]{3,2,0,1:T(4,128)}, f32[3,1,4,128]{3,2,0,1:T(4,128)S(1)}, u32[]{:S(2)}, u32[]{:S(2)}) collective-permute-start(f32[3,1,4,128]{3,2,0,1:T(4,128)} %bitcast.17), channel_id=1, source_target_pairs={{1,0},{2,1},{3,2},{4,3},{5,4},{6,5},{7,6},{8,7},{9,8},{10,9},{11,1... | collective-permute-start | bytes 18440 | tf_op jit(solution)/shard_map/ppermute | solution.py:27
  24.3 10.4 %collective-permute-start.1 = (f32[3,4,128]{2,1,0:T(4,128)S(1)}, f32[3,4,128]{2,1,0:T(4,128)S(1)}, u32[]{:S(2)}, u32[]{:S(2)}) collective-permute-start(f32[3,4,128]{2,1,0:T(4,128)S(1)} %get-tuple-element.36), channel_id=1, source_target_pairs={{0,1},{1,2},{2,3},{3,4},{4,5},{5,6},{6,7},{7,8},{8,9},{9,10},{10,1... | collective-permute-start | bytes 18440 | tf_op jit(solution)/shard_map/ppermute | solution.py:27

commit v6 on v5

--- a/solution.py
+++ b/solution.py
@@ -130,7 +130,7 @@
     slot_rows = lax.broadcasted_iota(jnp.int32, (32, 128), 0)
     for row in range(32):
         picked = jnp.broadcast_to(rank_ref[row : row + 1, :], (32, 128)) == slot_rows
-        sel_ref[:, row * 128 : (row + 1) * 128] = jnp.where(picked, 1.0, 0.0).astype(jnp.bfloat16)
+        sel_ref[row] = jnp.where(picked, 1.0, 0.0).astype(jnp.bfloat16)
 
     basis_ref[168:256, :] = jnp.zeros((88, 128), jnp.float32)
 
@@ -150,10 +150,9 @@
         for contact in range(CONTACTS):
             basis = basis_ref[pl.ds(contact, 32, stride=8), :]
             high = basis.astype(jnp.bfloat16)
-            split_ref[contact, 0:32, lanes] = high
-            split_ref[contact, 32:64, lanes] = (basis - high.astype(jnp.float32)).astype(
-                jnp.bfloat16
-            )
+            low = (basis - high.astype(jnp.float32)).astype(jnp.bfloat16)
+            split_ref[contact * CHUNKS + chunk, 0:32, :] = high
+            split_ref[contact * CHUNKS + chunk, 32:64, :] = low
         for slot in range(SLOT_COUNT):
             raw_ref[slot * 8 : (slot + 1) * 8, :] = (
                 stiff_ref[slot, :, lanes].astype(jnp.float32) * mask
@@ -175,7 +174,10 @@
     for contact in range(CONTACTS):
         weights = wt_ref[contact].astype(jnp.bfloat16)
         acc = acc + lax.dot_general(
-            split_ref[contact], weights, NT, preferred_element_type=jnp.float32
+            jnp.concatenate([split_ref[contact * CHUNKS + chunk] for chunk in range(CHUNKS)], axis=1),
+            weights,
+            NT,
+            preferred_element_type=jnp.float32,
         )
     acc = acc[0:32] + acc[32:64]
     slot_lane = lax.broadcasted_iota(jnp.int32, (32, 32), 1).astype(jnp.float32)
@@ -320,7 +322,7 @@
         split_low_ref[:, row * 128 : (row + 1) * 128] = (value - high.astype(jnp.float32)).astype(
             jnp.bfloat16
         )
-    sel = sel_ref[...]
+    sel = jnp.concatenate([sel_ref[row] for row in range(32)], axis=1)
     slot_strain = lax.dot_general(
         sel, split_high_ref[...], NT, preferred_element_type=jnp.float32
     ) + lax.dot_general(sel, split_low_ref[...], NT, preferred_element_type=jnp.float32)
@@ -331,9 +333,14 @@
         ]
         for group in range(GROUPS)
     ]
-    strain_t = lax.dot_general(
-        split_high_ref[...], sel, NT, preferred_element_type=jnp.float32
-    ) + lax.dot_general(split_low_ref[...], sel, NT, preferred_element_type=jnp.float32)
+    strain_table = jnp.zeros((32, 128), jnp.float32)
+    strain_lane = lax.broadcasted_iota(jnp.int32, (32, 128), 1)
+    for comp in range(6):
+        strain_table = jnp.where(
+            strain_lane == comp, slot_strain[:, comp : comp + 1], strain_table
+        )
+    strain_full = jnp.concatenate([strain_table, jnp.zeros((96, 128), jnp.float32)], axis=0)
+    strain_t = jnp.transpose(strain_full)[0:8, 0:32]
     sums_ref[...] = jnp.zeros((192, 128), jnp.float32)
 
     def first_step(chunk, carry):
@@ -616,7 +623,7 @@
             jax.ShapeDtypeStruct((SLOT_COUNT, GRAINS), f32),
             jax.ShapeDtypeStruct((21, SLOT_COUNT), f32),
             jax.ShapeDtypeStruct((32, 128), jnp.int32),
-            jax.ShapeDtypeStruct((SLOT_COUNT, 4096), jnp.bfloat16),
+            jax.ShapeDtypeStruct((32, SLOT_COUNT, 128), jnp.bfloat16),
             jax.ShapeDtypeStruct((6, CONTACTS, GRAINS), f32),
         )
         + tuple(jax.ShapeDtypeStruct(value.shape, value.dtype) for value in kept),
@@ -625,7 +632,7 @@
         scratch_shapes=[
             pltpu.VMEM((SLOT_COUNT * CONTACTS, 128), f32),
             pltpu.VMEM((256, 128), f32),
-            pltpu.VMEM((CONTACTS, 64, GRAINS), jnp.bfloat16),
+            pltpu.VMEM((CONTACTS * CHUNKS, 64, 128), jnp.bfloat16),
             pltpu.VMEM((32, 128), jnp.int32),
             pltpu.VMEM((SLOT_COUNT, CONTACTS, GRAINS), jnp.bfloat16),
             pltpu.VMEM((CONTACTS, GRAINS), f32),

time: 35.5 us -> 35.3 us (level)
  no operation moved by 1% of the time
where the time goes in v6:
time: 35.3 us; the launch traced here: 35 us
  Pallas kernels  17.9 us (51%)
  starting transfers between devices  8.02 us (23%)
  waiting for transfers between devices  7.79 us (22%)
  between operations  0.67 us (2%)
  other arithmetic  0.6 us (2%)
    pallas_call x1, Pallas kernels, run_relax(): pl.pallas_call(relax_kernel, out_shape=(jax.ShapeDtypeStruct((3, 4, 128),...  13.9 us
    ppermute x2, starting transfers between devices, shifted(): lax.ppermute(value, axis, [(source, source + steps) for source in range(l...  8.02 us
    ppermute x2, waiting for transfers between devices, shifted(): lax.ppermute(value, axis, [(source, source + steps) for source in range(l...  7.79 us
    pallas_call x1, Pallas kernels, run_template(): pl.pallas_call(template_kernel, out_shape=(jax.ShapeDtypeStruct((CONTACTS...  3.39 us
  transfers between devices with their start and end apart: 2, of which 1 were waited for; matrix products, arithmetic and copies ran while one was open for 0% of the time, Pallas kernels for 12%

profile of v6, /device:TPU:128, one launch (start us, length us, event | category | flops | bytes accessed | tf_op | source)
XLA Modules:
  0.0 35.0 jit_solution(838184419322079123)
XLA Ops:
  0.6 6.1 %collective-permute-start = (f32[3,1,4,128]{3,2,0,1:T(4,128)}, f32[3,1,4,128]{3,2,0,1:T(4,128)S(1)}, u32[]{:S(2)}, u32[]{:S(2)}) collective-permute-start(f32[3,1,4,128]{3,2,0,1:T(4,128)} %bitcast.17), channel_id=1, source_target_pairs={{1,0},{2,1},{3,2},{4,3},{5,4},{6,5},{7,6},{8,7},{9,8},{10,9},{11,1... | collective-permute-start | bytes 18440 | tf_op jit(solution)/shard_map/ppermute | solution.py:27
  6.7 3.4 %template.1 = (f32[8,32,2048]{2,1,0:T(8,128)S(1)}, f32[32,2048]{1,0:T(8,128)S(1)}, f32[21,32]{1,0:T(8,128)S(1)}, s32[32,128]{1,0:T(8,128)S(1)}, bf16[32,32,128]{...) custom-call(s32[32,128]{1,0:T(8,128)} %bitcast.15, ...), custom_call_target="tpu_custom_call" | custom-call | flops 40000000 | bytes 8000000 | tf_op jit(solution)/shard_map/template/pallas_call | solution.py:619
  10.1 0.0 collective-permute-done
  10.2 13.9 %relax.1 = (f32[3,4,128]{2,1,0:T(4,128)S(1)}, f32[192,128]{1,0:T(8,128)S(1)}, f32[6,32]{1,0:T(8,128)S(1)}) custom-call(f32[3,4,128]{2,1,0:T(4,128)S(1)} %get-tuple-element.22.disp_ref, f32[3,4,128]{2,1,0:T(4,128)S(1)} %bitcast.13, bf16[672,128]{1,0:T(8,128)(2,1)S(1)} %get-tuple-element.23.tangent_ref, s32[32,128]{1,0:T(8,128)S(1)} %get-tuple-element.24.rank_ref, ...), custom_call_target="tpu_custom_call" | custom-call | flops 200000000 | bytes 8000000 | tf_op jit(solution)/shard_map/relax/pallas_call | solution.py:655
  24.0 1.9 %collective-permute-start.1 = (f32[3,4,128]{2,1,0:T(4,128)S(1)}, f32[3,4,128]{2,1,0:T(4,128)S(1)}, u32[]{:S(2)}, u32[]{:S(2)}) collective-permute-start(f32[3,4,128]{2,1,0:T(4,128)S(1)} %get-tuple-element.36), channel_id=1, source_target_pairs={{0,1},{1,2},{2,3},{3,4},{4,5},{5,6},{6,7},{7,8},{8,9},{9,10},{10,1... | collective-permute-start | bytes 18440 | tf_op jit(solution)/shard_map/ppermute | solution.py:27
  26.0 0.7 %output.1 = (f32[3,4,128]{2,1,0:T(4,128)S(1)}, f32[192,128]{1,0:T(8,128)}, f32[6,32]{1,0:T(8,128)}, f32[21,32]{1,0:T(8,128)}) custom-call(f32[192,128]{1,0:T(8,128)S(1)} %get-tuple-element.32.stress_in, f32[6,32]{1,0:T(8,128)S(1)} %get-tuple-element.33.band_in, f32[21,32]{1,0:T(8,128)S(1)} %get-tuple-element.31.tan_ref.tan_in, ...), custom_call_target="tpu_custom_call" | custom-call | flops 1000000 | bytes 2000000 | tf_op jit(solution)/shard_map/output/pallas_call | solution.py:688
  26.6 7.8 %collective-permute-done.1 = f32[3,4,128]{2,1,0:T(4,128)S(1)} collective-permute-done((f32[3,4,128]{2,1,0:T(4,128)S(1)}, f32[3,4,128]{2,1,0:T(4,128)S(1)}, u32[]{:S(2)}, u32[]{:S(2)}) %collective-permute-start.1) | collective-permute-done | bytes 6176 | tf_op jit(solution)/shard_map/ppermute | solution.py:27
  34.4 0.6 %subtract_bitcast_fusion = f32[3,1,4,128]{3,2,1,0:T(4,128)} fusion(f32[3,4,128]{2,1,0:T(4,128)S(1)} %get-tuple-element.35, f32[3,4,128]{2,1,0:T(4,128)S(1)} %collective-permute-done.1), kind=kLoop, calls=%fused_computation | loop fusion | flops 1536 | bytes 18432
Async XLA Ops:
  0.6 9.5 %collective-permute-start = (f32[3,1,4,128]{3,2,0,1:T(4,128)}, f32[3,1,4,128]{3,2,0,1:T(4,128)S(1)}, u32[]{:S(2)}, u32[]{:S(2)}) collective-permute-start(f32[3,1,4,128]{3,2,0,1:T(4,128)} %bitcast.17), channel_id=1, source_target_pairs={{1,0},{2,1},{3,2},{4,3},{5,4},{6,5},{7,6},{8,7},{9,8},{10,9},{11,1... | collective-permute-start | bytes 18440 | tf_op jit(solution)/shard_map/ppermute | solution.py:27
  24.0 10.4 %collective-permute-start.1 = (f32[3,4,128]{2,1,0:T(4,128)S(1)}, f32[3,4,128]{2,1,0:T(4,128)S(1)}, u32[]{:S(2)}, u32[]{:S(2)}) collective-permute-start(f32[3,4,128]{2,1,0:T(4,128)S(1)} %get-tuple-element.36), channel_id=1, source_target_pairs={{0,1},{1,2},{2,3},{3,4},{4,5},{5,6},{6,7},{7,8},{8,9},{9,10},{10,1... | collective-permute-start | bytes 18440 | tf_op jit(solution)/shard_map/ppermute | solution.py:27
